TPU v7x, 256 devices: a whole 4x4x8 slice. The times are simulated.
256 devices in a mesh: seq: 64 (over y, x, z_hi, core), tp: 4 (over z_lo).
Axes of the slice: x: 4, y: 4, z: 8 (z_hi: 2, z_lo: 4; z = z_hi * 4 + z_lo), core: 2. Of those that a mesh axis runs over, the one named last changes fastest.
Arguments:
- tokens: bfloat16 [32768, 2048], P('seq'), may hold values from -6 to 6
- norm_gain: float32 [2048], replicated, may hold values from 0.1 to 1.9
- query_key_value_weight: bfloat16 [2048, 8, 384], P(None, 'tp'), may hold values from -8 to 8
- output_weight: bfloat16 [8, 256, 2048], P('tp'), may hold values from -0.75 to 0.75
- out_gain: float32 [2048], P('tp'), may hold values from 0.1 to 1.9
- seg_ids: int32 [32768], P('seq'), may hold values from 0 to 15, never falling along the last dimension, each value on 1 to 8192 neighbouring positions
- earlier_cache: bfloat16 [4096, 8, 2048], P('seq', 'tp'), may hold values from -6 to 6
- decode_owner: int32 [4096, 1], P('seq'), may hold values from 0 to 63; in each aligned block of 64 rows (0 to 63, 64 to 127, ...) at most 2 rows name the same one
Outputs:
- hidden_out: bfloat16 [32768, 2048], P('seq', 'tp')
- mlp_input: bfloat16 [32768, 2048], P('seq', 'tp')
- decode_layout_cache: bfloat16 [8192, 8, 2048], P('seq', 'tp')
Inputs may be any that keep to these rules, and one draw needn't show every extreme that they name: `seg_ids`: request ids never fall along the tokens; every request 0 to 15 holds 1 to 8192 tokens in a row, and one holds exactly 8192. `decode_owner`: among the 64 rows of one device (aligned blocks of 64 rows) no owner is named more than 2 times; some owner is named exactly 2 times in some block.
All inputs are finite; a program needn't handle non-finite values.
Results may differ from a plain program's by a relative error of at most 0.014.
The roundings to bfloat16 on the way count: a program that leaves them out, or rounds other values in their place, can miss the bound.
Values may be sent and summed in bfloat16 or wider, within the bound.
A program may use at most 64 MiB of HBM per device.

v0:
```python
import math

import jax
import jax.numpy as jnp
from jax import lax
from jax.sharding import PartitionSpec as P

HEAD_SIZE = 64
QUERY_PER_KEY = 4
REQS = 16


def passed_along(value, axis, by):
    length = lax.axis_size(axis)
    pairs = [(i, i + by) for i in range(length) if 0 <= i + by < length]
    return lax.ppermute(value, axis, pairs)


def norm_scale(cache_entries, gain_row):
    mean_square = jnp.mean(cache_entries * cache_entries, axis=-1, keepdims=True)
    return cache_entries * lax.rsqrt(mean_square + 1e-05) * gain_row


def angles(position, head_dim):
    half_dim = head_dim // 2
    frequency = jnp.exp(
        -(2.0 * jnp.arange(half_dim, dtype=jnp.float32) / head_dim) * math.log(500000.0)
    )
    return position.astype(jnp.float32)[:, None] * frequency[None, :]


def apply_rotary(cache_entries, rotary_phase):
    half_dim = cache_entries.shape[-1] // 2
    cosine = jnp.cos(rotary_phase)[:, None, :]
    sine_part = jnp.sin(rotary_phase)[:, None, :]
    first_half = cache_entries[..., :half_dim]
    second_half = cache_entries[..., half_dim:]
    return jnp.concatenate(
        [
            first_half * cosine - second_half * sine_part,
            second_half * cosine + first_half * sine_part,
        ],
        axis=-1,
    )


def per_device(
    tokens,
    norm_gain,
    query_key_value_weight,
    output_weight,
    out_gain,
    seg_ids,
    earlier_cache,
    decode_owner,
):
    tok_dev, model_width = tokens.shape
    kv_heads = query_key_value_weight.shape[1]
    seq_count = lax.axis_size("seq")
    tp_count = lax.axis_size("tp")
    offset = lax.axis_index("seq") * tok_dev
    values_in = tokens.astype(jnp.float32)
    normalized_input = norm_scale(values_in, norm_gain).astype(jnp.bfloat16)
    projected_rows = jnp.dot(
        normalized_input,
        query_key_value_weight.reshape(model_width, -1),
        preferred_element_type=jnp.float32,
    )
    projected_rows = projected_rows.reshape(tok_dev, kv_heads, QUERY_PER_KEY + 2, HEAD_SIZE)
    token_index = offset + jnp.arange(tok_dev, dtype=jnp.int32)
    request = jnp.arange(REQS, dtype=jnp.int32)
    member = seg_ids[:, None] == request[None, :]
    local_first = jnp.min(jnp.where(member, token_index[:, None], tok_dev * seq_count), axis=0)
    request_first = lax.pmin(local_first, "seq")
    position = token_index - jnp.sum(jnp.where(member, request_first[None, :], 0), axis=1)
    rotary_phase = angles(position, HEAD_SIZE)
    query_rows = apply_rotary(
        projected_rows[:, :, :QUERY_PER_KEY].reshape(tok_dev, kv_heads * QUERY_PER_KEY, HEAD_SIZE),
        rotary_phase,
    ) * HEAD_SIZE ** (-0.5)
    query_rows = query_rows.astype(jnp.bfloat16).reshape(
        tok_dev, kv_heads, QUERY_PER_KEY, HEAD_SIZE
    )
    key_rows = apply_rotary(projected_rows[:, :, QUERY_PER_KEY], rotary_phase).astype(jnp.bfloat16)
    values = projected_rows[:, :, QUERY_PER_KEY + 1].astype(jnp.bfloat16)
    packed = jnp.stack([key_rows, values], axis=2).reshape(tok_dev, kv_heads * 2 * HEAD_SIZE)
    query_last = offset + tok_dev - 1
    softmax_state = (
        jnp.full((kv_heads, QUERY_PER_KEY, tok_dev), -1e30, jnp.float32),
        jnp.zeros((kv_heads, QUERY_PER_KEY, tok_dev), jnp.float32),
        jnp.zeros((kv_heads, QUERY_PER_KEY, tok_dev, HEAD_SIZE), jnp.float32),
    )

    def absorb(carried, piece, piece_start):
        kv_piece, seg_piece = piece
        piece_rows = seg_piece.shape[0]
        key_index = piece_start + jnp.arange(piece_rows, dtype=jnp.int32)
        has_keys = (
            (piece_start >= 0)
            & (piece_start <= query_last)
            & (seg_piece[piece_rows - 1] >= seg_ids[0])
        )

        def attend_piece(inner_state):
            running_max, denominator, weighted_sum = inner_state
            unpacked = kv_piece.reshape(piece_rows, kv_heads, 2, HEAD_SIZE)
            scores = jnp.einsum(
                "qhgd,khd->hgqk", query_rows, unpacked[:, :, 0], preferred_element_type=jnp.float32
            )
            allowed = (
                (seg_ids[:, None] == seg_piece[None, :])
                & (key_index[None, :] <= token_index[:, None])
                & (key_index[None, :] >= 0)
            )
            scores = jnp.where(allowed, scores, -1e30)
            new_max = jnp.maximum(running_max, jnp.max(scores, axis=-1))
            weights = jnp.where(allowed, jnp.exp(scores - new_max[..., None]), 0.0)
            factor = jnp.exp(running_max - new_max)
            denominator = denominator * factor + jnp.sum(weights, axis=-1)
            weighted_sum = weighted_sum * factor[..., None] + jnp.einsum(
                "hgqk,khd->hgqd",
                weights.astype(jnp.bfloat16),
                unpacked[:, :, 1],
                preferred_element_type=jnp.float32,
            )
            return (new_max, denominator, weighted_sum)

        return lax.cond(has_keys, attend_piece, lambda inner_state: inner_state, carried)

    reach_blocks = min(seq_count - 1, (tok_dev * seq_count // 4 + tok_dev - 2) // tok_dev)
    softmax_state = absorb(softmax_state, (packed, seg_ids), offset)

    def advance(turn_index, carried):
        inner_state, moving, moving_seg = carried
        moving, moving_seg = passed_along((moving, moving_seg), "seq", 1)
        inner_state = absorb(inner_state, (moving, moving_seg), offset - (turn_index + 1) * tok_dev)
        return (inner_state, moving, moving_seg)

    result = lax.fori_loop(0, reach_blocks, advance, (softmax_state, packed, seg_ids))
    running_max, denominator, weighted_sum = result[0]
    attended = (weighted_sum / denominator[..., None]).astype(jnp.bfloat16)
    attended = jnp.transpose(attended, (2, 0, 1, 3)).reshape(
        tok_dev, kv_heads * QUERY_PER_KEY * HEAD_SIZE
    )
    projected_out = jnp.dot(
        attended, output_weight.reshape(-1, model_width), preferred_element_type=jnp.float32
    )
    share_width = model_width // tp_count
    column = lax.axis_index("tp") * share_width
    summed_all = values_in + lax.psum(projected_out.astype(jnp.bfloat16), "tp").astype(jnp.float32)
    mean_square = jnp.mean(summed_all * summed_all, axis=1)
    residual = lax.dynamic_slice_in_dim(summed_all, column, share_width, 1)
    hidden_out = residual.astype(jnp.bfloat16)
    mlp_input = (residual * lax.rsqrt(mean_square + 1e-05)[:, None] * out_gain).astype(jnp.bfloat16)
    blocks = earlier_cache.shape[0]
    slot_most = 2 * blocks // seq_count
    owner_index = decode_owner[:, 0]
    owner_hits = (owner_index[:, None] == jnp.arange(seq_count, dtype=jnp.int32)[None, :]).astype(
        jnp.int32
    )
    slot_rank = jnp.sum((jnp.cumsum(owner_hits, axis=0) - 1) * owner_hits, axis=1)
    decode_slot_row = owner_index * slot_most + slot_rank
    placement = (
        decode_slot_row[None, :] == jnp.arange(seq_count * slot_most, dtype=jnp.int32)[:, None]
    ).astype(jnp.bfloat16)
    outgoing = jnp.dot(
        placement, earlier_cache.reshape(blocks, -1), preferred_element_type=jnp.float32
    )
    outgoing = outgoing.astype(jnp.bfloat16).reshape(seq_count * slot_most, kv_heads, -1)
    decode_layout_cache = lax.all_to_all(outgoing, "seq", split_axis=0, concat_axis=0, tiled=True)
    return (hidden_out, mlp_input, decode_layout_cache)


def solution(mesh):
    in_specs = (
        P("seq", None),
        P(),
        P(None, "tp", None),
        P("tp", None, None),
        P("tp"),
        P("seq"),
        P("seq", "tp", None),
        P("seq", None),
    )
    out_specs = (P("seq", "tp"), P("seq", "tp"), P("seq", "tp", None))
    return jax.shard_map(
        per_device, mesh=mesh, in_specs=in_specs, out_specs=out_specs, check_vma=False
    )
```

profile of v0, /device:TPU:2, one launch (start us, length us, event | category | flops | bytes accessed | tf_op | source)
XLA Modules:
  0.0 594.6 jit_solution(8655280089801234312)
XLA Ops:
  7.3 4.3 copy.44
  11.6 4.7 copy.30
  18.4 4.4 fusion.34
  25.9 24.5 %pmin.7 = s32[16]{0:T(128)S(1)} all-reduce(s32[16]{0:T(128)S(1)} %select_reduce_fusion.2), channel_id=1, replica_groups=mesh['seq'=64,'tp'=4] {'seq'}, use_global_device_ids=true, to_apply=%region_2.3 | all-reduce | flops 16 | bytes 128 | tf_op jit(solution)/shard_map/pmin | solution.py:74
  52.4 8.7 %conditional.2 = (f32[2,4,512]{2,1,0:T(4,128)}, f32[2,4,512]{2,1,0:T(4,128)S(1)}, f32[2,4,512,64]{2,3,1,0:T(8,128)S(1)}) conditional(s32[]{:T(128)} %convert_element_type.74, () %tuple.37, (s32[512]{0:T(512)S(1)}, s32[512]{0:T(512)S(1)}, bf16[512,2,64]{0,2,1:T(8,128)(2,1)S(1)}, bf16[512,2,4,64]{0,3,2,1:T(8,128)(2,1)S(1)}, ...), branch_computations={%region_4.5_spmd, %region_5.8_spmd} | conditional | flops 559170048 | bytes 28236824 | solution.py:128
  54.7 2.5 fusion.4
  57.9 3.0 fusion.8
  62.1 287.3 %while.23 = (s32[]{:T(128)}, f32[2,4,512]{2,1,0:T(4,128)}, f32[2,4,512]{2,1,0:T(4,128)S(1)}, f32[2,4,512,64]{2,3,1,0:T(8,128)}, bf16[512,256]{0,1:T(8,128)(2,1)S...) while((s32[]{:T(128)}, f32[2,4,512]{2,1,0:T(4,128)}, ...), condition=%wide.region_13.14_spmd.clone.clone, body=%wide.region_8.13_spmd.clone.clone.sunk | while | flops 559425024 | bytes 39353832 | solution.py:139
  64.0 6.8 %collective-permute-start = (s32[512]{0:T(512)S(1)}, s32[512]{0:T(512)S(1)}, u32[]{:S(2)}, u32[]{:S(2)}) collective-permute-start(s32[512]{0:T(512)S(1)} %get-tuple-element.485), channel_id=1, source_target_pairs={{0,4},{4,8},{8,12},{12,16},{16,20},{20,24},{24,28},{28,32},{32,36}... | collective-permute-start | bytes 6152 | tf_op jit(solution)/shard_map/while/body/eval_jaxpr/ppermute | solution.py:16
  71.4 3.3 collective-permute-done
  76.6 9.0 %conditional.6 = ((f32[2,4,512]{2,1,0:T(4,128)}, f32[2,4,512]{2,1,0:T(4,128)S(1)}, f32[2,4,512,64]{2,3,1,0:T(8,128)})) conditional(s32[]{:T(128)} %convert_element_type.131, (f32[2,4,512]{2,1,0:T(4,128)}, f32[2,4,512]{2,1,0:T(4,128)S(1)}, f32[2,4,512,64]{2,3,1,0:T(8,128)}) %tuple.77, (s32[512]{0:T(512)S(1)}, s32[512]{0:T(512)S(1)}, s32[]{:T(128)}, ...), branch_computations={%region_9.9_spmd, %region_10.12_spmd} | conditional | flops 559425024 | bytes 37766240 | solution.py:128
  82.2 2.4 fusion.24
  87.5 6.6 %collective-permute-start = (s32[512]{0:T(512)S(1)}, s32[512]{0:T(512)S(1)}, u32[]{:S(2)}, u32[]{:S(2)}) collective-permute-start(s32[512]{0:T(512)S(1)} %get-tuple-element.485), channel_id=1, source_target_pairs={{0,4},{4,8},{8,12},{12,16},{16,20},{20,24},{24,28},{28,32},{32,36}... | collective-permute-start | bytes 6152 | tf_op jit(solution)/shard_map/while/body/eval_jaxpr/ppermute | solution.py:16
  94.7 3.5 collective-permute-done
  100.2 8.2 %collective-permute-start.1 = (bf16[512,256]{0,1:T(8,128)(2,1)S(1)}, bf16[512,256]{0,1:T(8,128)(2,1)S(1)}, u32[]{:S(2)}, u32[]{:S(2)}) collective-permute-start(bf16[512,256]{0,1:T(8,128)(2,1)S(1)} %get-tuple-element.484), channel_id=1, source_target_pairs={{0,4},{4,8},{8,12},{12,16},{16,20},{20,24},{24,28},{28,32},{32,36}... | collective-permute-start | bytes 786440 | tf_op jit(solution)/shard_map/while/body/eval_jaxpr/ppermute | solution.py:16
  108.5 8.3 %collective-permute-start = (s32[512]{0:T(512)S(1)}, s32[512]{0:T(512)S(1)}, u32[]{:S(2)}, u32[]{:S(2)}) collective-permute-start(s32[512]{0:T(512)S(1)} %get-tuple-element.485), channel_id=1, source_target_pairs={{0,4},{4,8},{8,12},{12,16},{16,20},{20,24},{24,28},{28,32},{32,36}... | collective-permute-start | bytes 6152 | tf_op jit(solution)/shard_map/while/body/eval_jaxpr/ppermute | solution.py:16
  122.3 17.0 %collective-permute-start = (s32[512]{0:T(512)S(1)}, s32[512]{0:T(512)S(1)}, u32[]{:S(2)}, u32[]{:S(2)}) collective-permute-start(s32[512]{0:T(512)S(1)} %get-tuple-element.485), channel_id=1, source_target_pairs={{0,4},{4,8},{8,12},{12,16},{16,20},{20,24},{24,28},{28,32},{32,36}... | collective-permute-start | bytes 6152 | tf_op jit(solution)/shard_map/while/body/eval_jaxpr/ppermute | solution.py:16
  142.0 2.5 collective-permute-start.1
  144.6 8.3 %collective-permute-start = (s32[512]{0:T(512)S(1)}, s32[512]{0:T(512)S(1)}, u32[]{:S(2)}, u32[]{:S(2)}) collective-permute-start(s32[512]{0:T(512)S(1)} %get-tuple-element.485), channel_id=1, source_target_pairs={{0,4},{4,8},{8,12},{12,16},{16,20},{20,24},{24,28},{28,32},{32,36}... | collective-permute-start | bytes 6152 | tf_op jit(solution)/shard_map/while/body/eval_jaxpr/ppermute | solution.py:16
  156.6 6.7 %collective-permute-start.1 = (bf16[512,256]{0,1:T(8,128)(2,1)S(1)}, bf16[512,256]{0,1:T(8,128)(2,1)S(1)}, u32[]{:S(2)}, u32[]{:S(2)}) collective-permute-start(bf16[512,256]{0,1:T(8,128)(2,1)S(1)} %get-tuple-element.484), channel_id=1, source_target_pairs={{0,4},{4,8},{8,12},{12,16},{16,20},{20,24},{24,28},{28,32},{32,36}... | collective-permute-start | bytes 786440 | tf_op jit(solution)/shard_map/while/body/eval_jaxpr/ppermute | solution.py:16
  163.3 9.3 %collective-permute-start = (s32[512]{0:T(512)S(1)}, s32[512]{0:T(512)S(1)}, u32[]{:S(2)}, u32[]{:S(2)}) collective-permute-start(s32[512]{0:T(512)S(1)} %get-tuple-element.485), channel_id=1, source_target_pairs={{0,4},{4,8},{8,12},{12,16},{16,20},{20,24},{24,28},{28,32},{32,36}... | collective-permute-start | bytes 6152 | tf_op jit(solution)/shard_map/while/body/eval_jaxpr/ppermute | solution.py:16
  175.4 2.5 collective-permute-start.1
  177.9 18.1 %collective-permute-start = (s32[512]{0:T(512)S(1)}, s32[512]{0:T(512)S(1)}, u32[]{:S(2)}, u32[]{:S(2)}) collective-permute-start(s32[512]{0:T(512)S(1)} %get-tuple-element.485), channel_id=1, source_target_pairs={{0,4},{4,8},{8,12},{12,16},{16,20},{20,24},{24,28},{28,32},{32,36}... | collective-permute-start | bytes 6152 | tf_op jit(solution)/shard_map/while/body/eval_jaxpr/ppermute | solution.py:16
  198.8 2.5 collective-permute-start.1
  201.3 9.2 %collective-permute-start = (s32[512]{0:T(512)S(1)}, s32[512]{0:T(512)S(1)}, u32[]{:S(2)}, u32[]{:S(2)}) collective-permute-start(s32[512]{0:T(512)S(1)} %get-tuple-element.485), channel_id=1, source_target_pairs={{0,4},{4,8},{8,12},{12,16},{16,20},{20,24},{24,28},{28,32},{32,36}... | collective-permute-start | bytes 6152 | tf_op jit(solution)/shard_map/while/body/eval_jaxpr/ppermute | solution.py:16
  213.3 5.6 collective-permute-start.1
  218.9 9.1 %collective-permute-start = (s32[512]{0:T(512)S(1)}, s32[512]{0:T(512)S(1)}, u32[]{:S(2)}, u32[]{:S(2)}) collective-permute-start(s32[512]{0:T(512)S(1)} %get-tuple-element.485), channel_id=1, source_target_pairs={{0,4},{4,8},{8,12},{12,16},{16,20},{20,24},{24,28},{28,32},{32,36}... | collective-permute-start | bytes 6152 | tf_op jit(solution)/shard_map/while/body/eval_jaxpr/ppermute | solution.py:16
  230.8 3.4 collective-permute-start.1
  234.2 15.8 %collective-permute-start = (s32[512]{0:T(512)S(1)}, s32[512]{0:T(512)S(1)}, u32[]{:S(2)}, u32[]{:S(2)}) collective-permute-start(s32[512]{0:T(512)S(1)} %get-tuple-element.485), channel_id=1, source_target_pairs={{0,4},{4,8},{8,12},{12,16},{16,20},{20,24},{24,28},{28,32},{32,36}... | collective-permute-start | bytes 6152 | tf_op jit(solution)/shard_map/while/body/eval_jaxpr/ppermute | solution.py:16
  252.8 2.5 collective-permute-start.1
  255.3 9.2 %collective-permute-start = (s32[512]{0:T(512)S(1)}, s32[512]{0:T(512)S(1)}, u32[]{:S(2)}, u32[]{:S(2)}) collective-permute-start(s32[512]{0:T(512)S(1)} %get-tuple-element.485), channel_id=1, source_target_pairs={{0,4},{4,8},{8,12},{12,16},{16,20},{20,24},{24,28},{28,32},{32,36}... | collective-permute-start | bytes 6152 | tf_op jit(solution)/shard_map/while/body/eval_jaxpr/ppermute | solution.py:16
  267.3 5.3 collective-permute-start.1
  272.5 9.4 %collective-permute-start = (s32[512]{0:T(512)S(1)}, s32[512]{0:T(512)S(1)}, u32[]{:S(2)}, u32[]{:S(2)}) collective-permute-start(s32[512]{0:T(512)S(1)} %get-tuple-element.485), channel_id=1, source_target_pairs={{0,4},{4,8},{8,12},{12,16},{16,20},{20,24},{24,28},{28,32},{32,36}... | collective-permute-start | bytes 6152 | tf_op jit(solution)/shard_map/while/body/eval_jaxpr/ppermute | solution.py:16
  284.7 3.4 collective-permute-start.1
  288.1 9.4 %collective-permute-start = (s32[512]{0:T(512)S(1)}, s32[512]{0:T(512)S(1)}, u32[]{:S(2)}, u32[]{:S(2)}) collective-permute-start(s32[512]{0:T(512)S(1)} %get-tuple-element.485), channel_id=1, source_target_pairs={{0,4},{4,8},{8,12},{12,16},{16,20},{20,24},{24,28},{28,32},{32,36}... | collective-permute-start | bytes 6152 | tf_op jit(solution)/shard_map/while/body/eval_jaxpr/ppermute | solution.py:16
  300.3 4.6 collective-permute-start.1
  304.9 9.4 %collective-permute-start = (s32[512]{0:T(512)S(1)}, s32[512]{0:T(512)S(1)}, u32[]{:S(2)}, u32[]{:S(2)}) collective-permute-start(s32[512]{0:T(512)S(1)} %get-tuple-element.485), channel_id=1, source_target_pairs={{0,4},{4,8},{8,12},{12,16},{16,20},{20,24},{24,28},{28,32},{32,36}... | collective-permute-start | bytes 6152 | tf_op jit(solution)/shard_map/while/body/eval_jaxpr/ppermute | solution.py:16
  317.0 3.9 collective-permute-start.1
  321.0 9.4 %collective-permute-start = (s32[512]{0:T(512)S(1)}, s32[512]{0:T(512)S(1)}, u32[]{:S(2)}, u32[]{:S(2)}) collective-permute-start(s32[512]{0:T(512)S(1)} %get-tuple-element.485), channel_id=1, source_target_pairs={{0,4},{4,8},{8,12},{12,16},{16,20},{20,24},{24,28},{28,32},{32,36}... | collective-permute-start | bytes 6152 | tf_op jit(solution)/shard_map/while/body/eval_jaxpr/ppermute | solution.py:16
  333.1 4.1 collective-permute-start.1
  337.2 9.4 %collective-permute-start = (s32[512]{0:T(512)S(1)}, s32[512]{0:T(512)S(1)}, u32[]{:S(2)}, u32[]{:S(2)}) collective-permute-start(s32[512]{0:T(512)S(1)} %get-tuple-element.485), channel_id=1, source_target_pairs={{0,4},{4,8},{8,12},{12,16},{16,20},{20,24},{24,28},{28,32},{32,36}... | collective-permute-start | bytes 6152 | tf_op jit(solution)/shard_map/while/body/eval_jaxpr/ppermute | solution.py:16
  350.7 2.6 convolution_convert_fusion.1
  355.3 2.6 reshape.186
  357.9 108.3 %all-to-all-start = ((bf16[128,2,2048]{2,1,0:T(2,128)(2,1)}), bf16[128,2,2048]{2,1,0:T(2,128)(2,1)}, u32[]{:S(2)}, u32[]{:S(2)}) async-start(bf16[128,2,2048]{2,1,0:T(2,128)(2,1)} %reshape.186), calls=%async_computation | async-start | bytes 2097152 | tf_op jit(solution)/shard_map/all_to_all | solution.py:170
  466.3 31.1 %all-to-all-done = bf16[128,2,2048]{2,1,0:T(2,128)(2,1)} async-done(((bf16[128,2,2048]{2,1,0:T(2,128)(2,1)}), bf16[128,2,2048]{2,1,0:T(2,128)(2,1)}, u32[]{:S(2)}, u32[]{:S(2)}) %all-to-all-start) | async-done | bytes 1048608 | tf_op jit(solution)/shard_map/all_to_all | solution.py:170
  497.4 82.7 %all-reduce.2.cloned.1.call-done = bf16[512,2048]{1,0:T(8,128)(2,1)} async-done(((bf16[512,2048]{1,0:T(8,128)(2,1)}), bf16[512,2048]{1,0:T(8,128)(2,1)}) %all-reduce.2.cloned.1.call-update) | async-done | bytes 2097168 | tf_op jit(solution)/shard_map/psum | solution.py:150
  580.1 3.0 multiply_reduce_fusion
  584.9 2.9 copy.78
  (189 shorter events, 51.6 us)
Async XLA Ops:
  7.2 343.6 %copy-start = (bf16[2,256,2048]{2,1,0:T(8,128)(2,1)S(1)}, bf16[2,256,2048]{2,1,0:T(8,128)(2,1)}, u32[]{:S(2)}) copy-start(bf16[2,256,2048]{2,1,0:T(8,128)(2,1)} %param.17) | copy-start | bytes 6291460
  7.2 572.9 %all-reduce.2.cloned.1.call-start = ((), (), s32[]{:S(2)}) async-start(), calls=%async_computation.1 | async-start | bytes 4194304 | tf_op jit(solution)/shard_map/psum | solution.py:150
  11.6 6.8 %copy-start.8 = (f32[2048]{0:T(1024)S(1)}, f32[2048]{0:T(1024)}, u32[]{:S(2)}) copy-start(f32[2048]{0:T(1024)} %param.15) | copy-start | bytes 24580
  18.4 5.5 copy-start.5
  61.1 1.0 copy-start.1
  62.1 14.5 %collective-permute-start.1 = (bf16[512,256]{0,1:T(8,128)(2,1)S(1)}, bf16[512,256]{0,1:T(8,128)(2,1)S(1)}, u32[]{:S(2)}, u32[]{:S(2)}) collective-permute-start(bf16[512,256]{0,1:T(8,128)(2,1)S(1)} %get-tuple-element.484), channel_id=1, source_target_pairs={{0,4},{4,8},{8,12},{12,16},{16,20},{20,24},{24,28},{28,32},{32,36}... | collective-permute-start | bytes 786440 | tf_op jit(solution)/shard_map/while/body/eval_jaxpr/ppermute | solution.py:16
  64.0 10.7 %collective-permute-start = (s32[512]{0:T(512)S(1)}, s32[512]{0:T(512)S(1)}, u32[]{:S(2)}, u32[]{:S(2)}) collective-permute-start(s32[512]{0:T(512)S(1)} %get-tuple-element.485), channel_id=1, source_target_pairs={{0,4},{4,8},{8,12},{12,16},{16,20},{20,24},{24,28},{28,32},{32,36}... | collective-permute-start | bytes 6152 | tf_op jit(solution)/shard_map/while/body/eval_jaxpr/ppermute | solution.py:16
  79.1 3.1 copy-start.2
  84.6 1.0 copy-start.3
  85.6 14.5 %collective-permute-start.1 = (bf16[512,256]{0,1:T(8,128)(2,1)S(1)}, bf16[512,256]{0,1:T(8,128)(2,1)S(1)}, u32[]{:S(2)}, u32[]{:S(2)}) collective-permute-start(bf16[512,256]{0,1:T(8,128)(2,1)S(1)} %get-tuple-element.484), channel_id=1, source_target_pairs={{0,4},{4,8},{8,12},{12,16},{16,20},{20,24},{24,28},{28,32},{32,36}... | collective-permute-start | bytes 786440 | tf_op jit(solution)/shard_map/while/body/eval_jaxpr/ppermute | solution.py:16
  87.5 10.7 %collective-permute-start = (s32[512]{0:T(512)S(1)}, s32[512]{0:T(512)S(1)}, u32[]{:S(2)}, u32[]{:S(2)}) collective-permute-start(s32[512]{0:T(512)S(1)} %get-tuple-element.485), channel_id=1, source_target_pairs={{0,4},{4,8},{8,12},{12,16},{16,20},{20,24},{24,28},{28,32},{32,36}... | collective-permute-start | bytes 6152 | tf_op jit(solution)/shard_map/while/body/eval_jaxpr/ppermute | solution.py:16
  100.2 20.1 %collective-permute-start.1 = (bf16[512,256]{0,1:T(8,128)(2,1)S(1)}, bf16[512,256]{0,1:T(8,128)(2,1)S(1)}, u32[]{:S(2)}, u32[]{:S(2)}) collective-permute-start(bf16[512,256]{0,1:T(8,128)(2,1)S(1)} %get-tuple-element.484), channel_id=1, source_target_pairs={{0,4},{4,8},{8,12},{12,16},{16,20},{20,24},{24,28},{28,32},{32,36}... | collective-permute-start | bytes 786440 | tf_op jit(solution)/shard_map/while/body/eval_jaxpr/ppermute | solution.py:16
  108.5 9.9 %collective-permute-start = (s32[512]{0:T(512)S(1)}, s32[512]{0:T(512)S(1)}, u32[]{:S(2)}, u32[]{:S(2)}) collective-permute-start(s32[512]{0:T(512)S(1)} %get-tuple-element.485), channel_id=1, source_target_pairs={{0,4},{4,8},{8,12},{12,16},{16,20},{20,24},{24,28},{28,32},{32,36}... | collective-permute-start | bytes 6152 | tf_op jit(solution)/shard_map/while/body/eval_jaxpr/ppermute | solution.py:16
  120.4 21.6 %collective-permute-start.1 = (bf16[512,256]{0,1:T(8,128)(2,1)S(1)}, bf16[512,256]{0,1:T(8,128)(2,1)S(1)}, u32[]{:S(2)}, u32[]{:S(2)}) collective-permute-start(bf16[512,256]{0,1:T(8,128)(2,1)S(1)} %get-tuple-element.484), channel_id=1, source_target_pairs={{0,4},{4,8},{8,12},{12,16},{16,20},{20,24},{24,28},{28,32},{32,36}... | collective-permute-start | bytes 786440 | tf_op jit(solution)/shard_map/while/body/eval_jaxpr/ppermute | solution.py:16
  122.3 17.8 %collective-permute-start = (s32[512]{0:T(512)S(1)}, s32[512]{0:T(512)S(1)}, u32[]{:S(2)}, u32[]{:S(2)}) collective-permute-start(s32[512]{0:T(512)S(1)} %get-tuple-element.485), channel_id=1, source_target_pairs={{0,4},{4,8},{8,12},{12,16},{16,20},{20,24},{24,28},{28,32},{32,36}... | collective-permute-start | bytes 6152 | tf_op jit(solution)/shard_map/while/body/eval_jaxpr/ppermute | solution.py:16
  142.0 14.4 %collective-permute-start.1 = (bf16[512,256]{0,1:T(8,128)(2,1)S(1)}, bf16[512,256]{0,1:T(8,128)(2,1)S(1)}, u32[]{:S(2)}, u32[]{:S(2)}) collective-permute-start(bf16[512,256]{0,1:T(8,128)(2,1)S(1)} %get-tuple-element.484), channel_id=1, source_target_pairs={{0,4},{4,8},{8,12},{12,16},{16,20},{20,24},{24,28},{28,32},{32,36}... | collective-permute-start | bytes 786440 | tf_op jit(solution)/shard_map/while/body/eval_jaxpr/ppermute | solution.py:16
  144.6 10.0 %collective-permute-start = (s32[512]{0:T(512)S(1)}, s32[512]{0:T(512)S(1)}, u32[]{:S(2)}, u32[]{:S(2)}) collective-permute-start(s32[512]{0:T(512)S(1)} %get-tuple-element.485), channel_id=1, source_target_pairs={{0,4},{4,8},{8,12},{12,16},{16,20},{20,24},{24,28},{28,32},{32,36}... | collective-permute-start | bytes 6152 | tf_op jit(solution)/shard_map/while/body/eval_jaxpr/ppermute | solution.py:16
  156.6 18.7 %collective-permute-start.1 = (bf16[512,256]{0,1:T(8,128)(2,1)S(1)}, bf16[512,256]{0,1:T(8,128)(2,1)S(1)}, u32[]{:S(2)}, u32[]{:S(2)}) collective-permute-start(bf16[512,256]{0,1:T(8,128)(2,1)S(1)} %get-tuple-element.484), channel_id=1, source_target_pairs={{0,4},{4,8},{8,12},{12,16},{16,20},{20,24},{24,28},{28,32},{32,36}... | collective-permute-start | bytes 786440 | tf_op jit(solution)/shard_map/while/body/eval_jaxpr/ppermute | solution.py:16
  163.3 10.1 %collective-permute-start = (s32[512]{0:T(512)S(1)}, s32[512]{0:T(512)S(1)}, u32[]{:S(2)}, u32[]{:S(2)}) collective-permute-start(s32[512]{0:T(512)S(1)} %get-tuple-element.485), channel_id=1, source_target_pairs={{0,4},{4,8},{8,12},{12,16},{16,20},{20,24},{24,28},{28,32},{32,36}... | collective-permute-start | bytes 6152 | tf_op jit(solution)/shard_map/while/body/eval_jaxpr/ppermute | solution.py:16
  175.4 23.3 %collective-permute-start.1 = (bf16[512,256]{0,1:T(8,128)(2,1)S(1)}, bf16[512,256]{0,1:T(8,128)(2,1)S(1)}, u32[]{:S(2)}, u32[]{:S(2)}) collective-permute-start(bf16[512,256]{0,1:T(8,128)(2,1)S(1)} %get-tuple-element.484), channel_id=1, source_target_pairs={{0,4},{4,8},{8,12},{12,16},{16,20},{20,24},{24,28},{28,32},{32,36}... | collective-permute-start | bytes 786440 | tf_op jit(solution)/shard_map/while/body/eval_jaxpr/ppermute | solution.py:16
  177.9 18.9 %collective-permute-start = (s32[512]{0:T(512)S(1)}, s32[512]{0:T(512)S(1)}, u32[]{:S(2)}, u32[]{:S(2)}) collective-permute-start(s32[512]{0:T(512)S(1)} %get-tuple-element.485), channel_id=1, source_target_pairs={{0,4},{4,8},{8,12},{12,16},{16,20},{20,24},{24,28},{28,32},{32,36}... | collective-permute-start | bytes 6152 | tf_op jit(solution)/shard_map/while/body/eval_jaxpr/ppermute | solution.py:16
  198.8 14.4 %collective-permute-start.1 = (bf16[512,256]{0,1:T(8,128)(2,1)S(1)}, bf16[512,256]{0,1:T(8,128)(2,1)S(1)}, u32[]{:S(2)}, u32[]{:S(2)}) collective-permute-start(bf16[512,256]{0,1:T(8,128)(2,1)S(1)} %get-tuple-element.484), channel_id=1, source_target_pairs={{0,4},{4,8},{8,12},{12,16},{16,20},{20,24},{24,28},{28,32},{32,36}... | collective-permute-start | bytes 786440 | tf_op jit(solution)/shard_map/while/body/eval_jaxpr/ppermute | solution.py:16
  201.3 10.0 %collective-permute-start = (s32[512]{0:T(512)S(1)}, s32[512]{0:T(512)S(1)}, u32[]{:S(2)}, u32[]{:S(2)}) collective-permute-start(s32[512]{0:T(512)S(1)} %get-tuple-element.485), channel_id=1, source_target_pairs={{0,4},{4,8},{8,12},{12,16},{16,20},{20,24},{24,28},{28,32},{32,36}... | collective-permute-start | bytes 6152 | tf_op jit(solution)/shard_map/while/body/eval_jaxpr/ppermute | solution.py:16
  213.3 17.4 %collective-permute-start.1 = (bf16[512,256]{0,1:T(8,128)(2,1)S(1)}, bf16[512,256]{0,1:T(8,128)(2,1)S(1)}, u32[]{:S(2)}, u32[]{:S(2)}) collective-permute-start(bf16[512,256]{0,1:T(8,128)(2,1)S(1)} %get-tuple-element.484), channel_id=1, source_target_pairs={{0,4},{4,8},{8,12},{12,16},{16,20},{20,24},{24,28},{28,32},{32,36}... | collective-permute-start | bytes 786440 | tf_op jit(solution)/shard_map/while/body/eval_jaxpr/ppermute | solution.py:16
  218.9 9.9 %collective-permute-start = (s32[512]{0:T(512)S(1)}, s32[512]{0:T(512)S(1)}, u32[]{:S(2)}, u32[]{:S(2)}) collective-permute-start(s32[512]{0:T(512)S(1)} %get-tuple-element.485), channel_id=1, source_target_pairs={{0,4},{4,8},{8,12},{12,16},{16,20},{20,24},{24,28},{28,32},{32,36}... | collective-permute-start | bytes 6152 | tf_op jit(solution)/shard_map/while/body/eval_jaxpr/ppermute | solution.py:16
  230.8 21.9 %collective-permute-start.1 = (bf16[512,256]{0,1:T(8,128)(2,1)S(1)}, bf16[512,256]{0,1:T(8,128)(2,1)S(1)}, u32[]{:S(2)}, u32[]{:S(2)}) collective-permute-start(bf16[512,256]{0,1:T(8,128)(2,1)S(1)} %get-tuple-element.484), channel_id=1, source_target_pairs={{0,4},{4,8},{8,12},{12,16},{16,20},{20,24},{24,28},{28,32},{32,36}... | collective-permute-start | bytes 786440 | tf_op jit(solution)/shard_map/while/body/eval_jaxpr/ppermute | solution.py:16
  234.2 16.6 %collective-permute-start = (s32[512]{0:T(512)S(1)}, s32[512]{0:T(512)S(1)}, u32[]{:S(2)}, u32[]{:S(2)}) collective-permute-start(s32[512]{0:T(512)S(1)} %get-tuple-element.485), channel_id=1, source_target_pairs={{0,4},{4,8},{8,12},{12,16},{16,20},{20,24},{24,28},{28,32},{32,36}... | collective-permute-start | bytes 6152 | tf_op jit(solution)/shard_map/while/body/eval_jaxpr/ppermute | solution.py:16
  252.8 14.4 %collective-permute-start.1 = (bf16[512,256]{0,1:T(8,128)(2,1)S(1)}, bf16[512,256]{0,1:T(8,128)(2,1)S(1)}, u32[]{:S(2)}, u32[]{:S(2)}) collective-permute-start(bf16[512,256]{0,1:T(8,128)(2,1)S(1)} %get-tuple-element.484), channel_id=1, source_target_pairs={{0,4},{4,8},{8,12},{12,16},{16,20},{20,24},{24,28},{28,32},{32,36}... | collective-permute-start | bytes 786440 | tf_op jit(solution)/shard_map/while/body/eval_jaxpr/ppermute | solution.py:16
  255.3 10.0 %collective-permute-start = (s32[512]{0:T(512)S(1)}, s32[512]{0:T(512)S(1)}, u32[]{:S(2)}, u32[]{:S(2)}) collective-permute-start(s32[512]{0:T(512)S(1)} %get-tuple-element.485), channel_id=1, source_target_pairs={{0,4},{4,8},{8,12},{12,16},{16,20},{20,24},{24,28},{28,32},{32,36}... | collective-permute-start | bytes 6152 | tf_op jit(solution)/shard_map/while/body/eval_jaxpr/ppermute | solution.py:16
  267.3 17.4 %collective-permute-start.1 = (bf16[512,256]{0,1:T(8,128)(2,1)S(1)}, bf16[512,256]{0,1:T(8,128)(2,1)S(1)}, u32[]{:S(2)}, u32[]{:S(2)}) collective-permute-start(bf16[512,256]{0,1:T(8,128)(2,1)S(1)} %get-tuple-element.484), channel_id=1, source_target_pairs={{0,4},{4,8},{8,12},{12,16},{16,20},{20,24},{24,28},{28,32},{32,36}... | collective-permute-start | bytes 786440 | tf_op jit(solution)/shard_map/while/body/eval_jaxpr/ppermute | solution.py:16
  272.5 10.2 %collective-permute-start = (s32[512]{0:T(512)S(1)}, s32[512]{0:T(512)S(1)}, u32[]{:S(2)}, u32[]{:S(2)}) collective-permute-start(s32[512]{0:T(512)S(1)} %get-tuple-element.485), channel_id=1, source_target_pairs={{0,4},{4,8},{8,12},{12,16},{16,20},{20,24},{24,28},{28,32},{32,36}... | collective-permute-start | bytes 6152 | tf_op jit(solution)/shard_map/while/body/eval_jaxpr/ppermute | solution.py:16
  284.7 15.5 %collective-permute-start.1 = (bf16[512,256]{0,1:T(8,128)(2,1)S(1)}, bf16[512,256]{0,1:T(8,128)(2,1)S(1)}, u32[]{:S(2)}, u32[]{:S(2)}) collective-permute-start(bf16[512,256]{0,1:T(8,128)(2,1)S(1)} %get-tuple-element.484), channel_id=1, source_target_pairs={{0,4},{4,8},{8,12},{12,16},{16,20},{20,24},{24,28},{28,32},{32,36}... | collective-permute-start | bytes 786440 | tf_op jit(solution)/shard_map/while/body/eval_jaxpr/ppermute | solution.py:16
  288.1 10.2 %collective-permute-start = (s32[512]{0:T(512)S(1)}, s32[512]{0:T(512)S(1)}, u32[]{:S(2)}, u32[]{:S(2)}) collective-permute-start(s32[512]{0:T(512)S(1)} %get-tuple-element.485), channel_id=1, source_target_pairs={{0,4},{4,8},{8,12},{12,16},{16,20},{20,24},{24,28},{28,32},{32,36}... | collective-permute-start | bytes 6152 | tf_op jit(solution)/shard_map/while/body/eval_jaxpr/ppermute | solution.py:16
  300.3 16.7 %collective-permute-start.1 = (bf16[512,256]{0,1:T(8,128)(2,1)S(1)}, bf16[512,256]{0,1:T(8,128)(2,1)S(1)}, u32[]{:S(2)}, u32[]{:S(2)}) collective-permute-start(bf16[512,256]{0,1:T(8,128)(2,1)S(1)} %get-tuple-element.484), channel_id=1, source_target_pairs={{0,4},{4,8},{8,12},{12,16},{16,20},{20,24},{24,28},{28,32},{32,36}... | collective-permute-start | bytes 786440 | tf_op jit(solution)/shard_map/while/body/eval_jaxpr/ppermute | solution.py:16
  304.9 10.2 %collective-permute-start = (s32[512]{0:T(512)S(1)}, s32[512]{0:T(512)S(1)}, u32[]{:S(2)}, u32[]{:S(2)}) collective-permute-start(s32[512]{0:T(512)S(1)} %get-tuple-element.485), channel_id=1, source_target_pairs={{0,4},{4,8},{8,12},{12,16},{16,20},{20,24},{24,28},{28,32},{32,36}... | collective-permute-start | bytes 6152 | tf_op jit(solution)/shard_map/while/body/eval_jaxpr/ppermute | solution.py:16
  317.0 16.0 %collective-permute-start.1 = (bf16[512,256]{0,1:T(8,128)(2,1)S(1)}, bf16[512,256]{0,1:T(8,128)(2,1)S(1)}, u32[]{:S(2)}, u32[]{:S(2)}) collective-permute-start(bf16[512,256]{0,1:T(8,128)(2,1)S(1)} %get-tuple-element.484), channel_id=1, source_target_pairs={{0,4},{4,8},{8,12},{12,16},{16,20},{20,24},{24,28},{28,32},{32,36}... | collective-permute-start | bytes 786440 | tf_op jit(solution)/shard_map/while/body/eval_jaxpr/ppermute | solution.py:16
  321.0 10.2 %collective-permute-start = (s32[512]{0:T(512)S(1)}, s32[512]{0:T(512)S(1)}, u32[]{:S(2)}, u32[]{:S(2)}) collective-permute-start(s32[512]{0:T(512)S(1)} %get-tuple-element.485), channel_id=1, source_target_pairs={{0,4},{4,8},{8,12},{12,16},{16,20},{20,24},{24,28},{28,32},{32,36}... | collective-permute-start | bytes 6152 | tf_op jit(solution)/shard_map/while/body/eval_jaxpr/ppermute | solution.py:16
  333.1 16.2 %collective-permute-start.1 = (bf16[512,256]{0,1:T(8,128)(2,1)S(1)}, bf16[512,256]{0,1:T(8,128)(2,1)S(1)}, u32[]{:S(2)}, u32[]{:S(2)}) collective-permute-start(bf16[512,256]{0,1:T(8,128)(2,1)S(1)} %get-tuple-element.484), channel_id=1, source_target_pairs={{0,4},{4,8},{8,12},{12,16},{16,20},{20,24},{24,28},{28,32},{32,36}... | collective-permute-start | bytes 786440 | tf_op jit(solution)/shard_map/while/body/eval_jaxpr/ppermute | solution.py:16
  337.2 10.2 %collective-permute-start = (s32[512]{0:T(512)S(1)}, s32[512]{0:T(512)S(1)}, u32[]{:S(2)}, u32[]{:S(2)}) collective-permute-start(s32[512]{0:T(512)S(1)} %get-tuple-element.485), channel_id=1, source_target_pairs={{0,4},{4,8},{8,12},{12,16},{16,20},{20,24},{24,28},{28,32},{32,36}... | collective-permute-start | bytes 6152 | tf_op jit(solution)/shard_map/while/body/eval_jaxpr/ppermute | solution.py:16
  350.7 2.6 copy-start.4
  350.7 2.8 copy-start.7
  357.9 139.5 %all-to-all-start = ((bf16[128,2,2048]{2,1,0:T(2,128)(2,1)}), bf16[128,2,2048]{2,1,0:T(2,128)(2,1)}, u32[]{:S(2)}, u32[]{:S(2)}) async-start(bf16[128,2,2048]{2,1,0:T(2,128)(2,1)} %reshape.186), calls=%async_computation | async-start | bytes 2097152 | tf_op jit(solution)/shard_map/all_to_all | solution.py:170
  466.3 117.7 %copy-start.6 = (f32[512]{0:T(512)S(1)}, f32[512]{0:T(512)}, u32[]{:S(2)}) copy-start(f32[512]{0:T(512)} %param.18) | copy-start | bytes 6148
Sparse Core Ops, SparseCore 0:
  353.5 226.5 all-reduce.1
where the time goes:
time: 600 us; the launch traced here: 595 us
  starting transfers between devices  334 us (56%)
  waiting for transfers between devices  125 us (21%)
  local copies, waits for them, and re-layouts  39.2 us (7%)
  blocking collectives  24.5 us (4%)
  loops' own time  22.3 us (4%)
  other arithmetic  17.5 us (3%)
  matrix products  16.6 us (3%)
  between operations  15.5 us (3%)
    ppermute x32, starting transfers between devices, passed_along(): return lax.ppermute(value, axis, pairs)  225 us
    all_to_all x1, starting transfers between devices, per_device(): lax.all_to_all(outgoing, 'seq', split_axis=0, concat_axis=0, tiled=True)  108 us
    psum x1, waiting for transfers between devices, per_device(): lax.psum(projected_out.astype(jnp.bfloat16), 'tp').astype(jnp.float32)  82.7 us
    all_to_all x1, waiting for transfers between devices, per_device(): lax.all_to_all(outgoing, 'seq', split_axis=0, concat_axis=0, tiled=True)  31.1 us
    pmin x1, blocking collectives, per_device(): request_first = lax.pmin(local_first, 'seq')  24.5 us
    another operation x1, loops' own time, per_device(): lax.fori_loop(0, reach_blocks, advance, (softmax_state, packed, seg_ids))  21.8 us
  transfers between devices with their start and end apart: 34, of which 18 were waited for; matrix products, arithmetic and copies ran while one was open for 4% of the time, Pallas kernels for 0%

commit v1 on v0

v1 whole, which is shorter than its diff:
```python
import functools
import math

import jax
import jax.numpy as jnp
import numpy as np
from jax import lax
from jax.experimental import pallas as pl
from jax.experimental.pallas import tpu as pltpu
from jax.sharding import PartitionSpec as P

HEAD_SIZE = 64
QUERY_PER_KEY = 4
REQS = 16
BIG = float(2.0**100)
CHUNKS = 4
PACKET_ROWS = 512 + 4 * 144
PAIRS = 8
EARLY_PAIRS = 5
MESH = pl.DeviceIdType.MESH
F32 = jnp.float32
BF16 = jnp.bfloat16


def rope_tables(tok, blocks):
    half = HEAD_SIZE // 2
    freq = 500000.0 ** (-2.0 * np.arange(half) / HEAD_SIZE)
    inner = freq[:, None] * np.arange(tok)[None, :]
    outer = freq[:, None] * (np.arange(128) * tok)[None, :]
    parts = [np.cos(inner), np.sin(inner), np.cos(outer), np.sin(outer)]
    return np.concatenate(parts, axis=1).astype(np.float32)


def body(
    n_seq,
    n_tp,
    x_hbm,
    gain_ref,
    w_hbm,
    wo_hbm,
    ogain_ref,
    seg_ref,
    cache_hbm,
    inv_ref,
    rope_ref,
    hid_ref,
    mlp_ref,
    dec_hbm,
    xv,
    wv,
    wov,
    cachev,
    outg,
    kvb,
    kf,
    qt,
    mx,
    acc,
    resid,
    rs_send,
    rs_recv,
    ss_send,
    ss_recv,
    lsem,
    c_ssem,
    c_rsem,
    kv_ssem,
    kv_rsem,
    r_ssem,
    r_rsem,
    s_ssem,
    s_rsem,
):
    me = lax.axis_index("seq")
    tp = lax.axis_index("tp")
    core = lax.rem(me, 2)
    zh = lax.rem(me // 2, 2)
    xx = lax.rem(me // 4, 4)
    slab = (me // 16) * 16
    tok = 512

    cp_cache = pltpu.make_async_copy(cache_hbm, cachev.at[pl.ds(0, 64)], lsem.at[0])
    cp_x = pltpu.make_async_copy(x_hbm, xv, lsem.at[1])
    cp_w = pltpu.make_async_copy(w_hbm, wv, lsem.at[2])
    cp_wo = pltpu.make_async_copy(wo_hbm, wov, lsem.at[3])
    cp_cache.start()
    cp_x.start()
    cp_w.start()
    cp_wo.start()

    barrier = pltpu.get_barrier_semaphore()

    def greet(k, carry):
        pl.semaphore_signal(
            barrier,
            inc=1,
            device_id={"seq": lax.rem(me + k, n_seq), "tp": tp},
            device_id_type=MESH,
        )
        return carry

    lax.fori_loop(1, n_seq, greet, 0)
    for k in range(1, n_tp):
        pl.semaphore_signal(
            barrier,
            inc=1,
            device_id={"seq": me, "tp": lax.rem(tp + k, n_tp)},
            device_id_type=MESH,
        )

    cachev[64] = jnp.zeros((2, 2048), BF16)
    cp_cache.wait()

    def place(r, carry):
        outg[r] = cachev[inv_ref[r]]
        return carry

    lax.fori_loop(0, 2 * n_seq, place, 0)
    pl.semaphore_wait(barrier, n_seq - 1 + n_tp - 1)

    def cache_copy(k):
        to = lax.rem(me + k, n_seq)
        return pltpu.make_async_remote_copy(
            src_ref=outg.at[pl.ds(2 * to, 2)],
            dst_ref=dec_hbm.at[pl.ds(2 * me, 2)],
            send_sem=c_ssem.at[k],
            recv_sem=c_rsem.at[k],
            device_id={"seq": to, "tp": tp},
            device_id_type=MESH,
        )

    def cache_start(k, carry):
        cache_copy(k).start()
        return carry

    lax.fori_loop(1, n_seq, cache_start, 0)
    cp_own = pltpu.make_async_copy(
        outg.at[pl.ds(2 * me, 2)], dec_hbm.at[pl.ds(2 * me, 2)], lsem.at[4]
    )
    cp_own.start()

    lane = lax.broadcasted_iota(jnp.int32, (32, 128), 1)
    here = lane == me
    cos_b = jnp.sum(jnp.where(here, rope_ref[:, 2 * tok : 2 * tok + 128], 0.0), axis=1, keepdims=True)
    sin_b = jnp.sum(
        jnp.where(here, rope_ref[:, 2 * tok + 128 : 2 * tok + 256], 0.0), axis=1, keepdims=True
    )
    q_scale = HEAD_SIZE ** (-0.5) * math.log2(math.e)

    seg = seg_ref[...].astype(F32)
    seg0 = jnp.min(seg, axis=1, keepdims=True)
    carried_in = seg == seg0
    first = jnp.zeros((1, tok), F32)
    for r in range(1, REQS):
        below = jnp.sum(jnp.where(seg < r, 1.0, 0.0), axis=1, keepdims=True)
        first = jnp.where(seg == r, below, first)
    a_bias = jnp.where(carried_in, 0.0, -BIG)

    row16 = lax.broadcasted_iota(jnp.int32, (16, 512), 0)
    for c in range(CHUNKS):
        ab = a_bias[:, c * 128 : (c + 1) * 128]
        ab4 = jnp.concatenate([ab, ab, ab, ab], axis=1)
        feat = jnp.where(row16 == 0, ab4, jnp.where(row16 == 1, 1.0, 0.0)).astype(BF16)
        for kv in range(2):
            at = kv * 2048 + c * 512
            qt[128:144, at : at + 512] = feat
            qt[144:256, at : at + 512] = jnp.zeros((112, 512), BF16)
            qt[(1 - kv) * 64 : (1 - kv) * 64 + 64, at : at + 512] = jnp.zeros((64, 512), BF16)

    cp_x.wait()
    cp_w.wait()
    gain = gain_ref[...]
    aux_row = lax.broadcasted_iota(jnp.int32, (16, 128), 0)
    for c in range(CHUNKS):
        cols = slice(c * 128, (c + 1) * 128)
        xc = xv[cols, :].astype(F32)
        ms = jnp.mean(xc * xc, axis=1, keepdims=True)
        normed = (xc * lax.rsqrt(ms + 1e-05) * gain).astype(BF16)
        proj = jnp.dot(normed, wv[...], preferred_element_type=F32)
        ci = rope_ref[:, c * 128 : (c + 1) * 128]
        si = rope_ref[:, tok + c * 128 : tok + (c + 1) * 128]
        cos = ci * cos_b - si * sin_b
        sin = si * cos_b + ci * sin_b
        cos_q, sin_q = cos * q_scale, sin * q_scale

        def rot(a, co, sn):
            a1, a2 = a[0:32], a[32:64]
            return jnp.concatenate([a1 * co - a2 * sn, a2 * co + a1 * sn], axis=0)

        keys, vals = [], []
        for kv in range(2):
            for pair in range(2):
                at = kv * 384 + pair * 128
                tr = jnp.transpose(proj[:, at : at + 128])
                for g2 in range(2):
                    g = pair * 2 + g2
                    lane0 = kv * 2048 + c * 512 + g * 128
                    qt[kv * 64 : kv * 64 + 64, lane0 : lane0 + 128] = rot(
                        tr[g2 * 64 : g2 * 64 + 64], cos_q, sin_q
                    ).astype(BF16)
            tr = jnp.transpose(proj[:, kv * 384 + 256 : kv * 384 + 384])
            keys.append(rot(tr[0:64], cos, sin))
            vals.append(tr[64:128].astype(BF16))
        kvb[0, c * 128 : (c + 1) * 128, :] = jnp.transpose(
            jnp.concatenate(keys, axis=0)
        ).astype(BF16)
        aux = jnp.where(
            aux_row == 0, 1.0, jnp.where(aux_row == 1, seg[:, c * 128 : (c + 1) * 128], 0.0)
        ).astype(BF16)
        base = 512 + c * 144
        kvb[0, base : base + 64, :] = vals[0]
        kvb[0, base + 64 : base + 80, :] = aux
        kvb[0, base + 80 : base + 144, :] = vals[1]

    def packet(src, dst, sem, seq_to):
        return pltpu.make_async_remote_copy(
            src_ref=kvb.at[src],
            dst_ref=kvb.at[dst],
            send_sem=kv_ssem.at[sem],
            recv_sem=kv_rsem.at[dst],
            device_id={"seq": seq_to, "tp": tp},
            device_id_type=MESH,
        )

    a1 = jnp.where(zh == 1, 9, 17)
    b1 = jnp.where(zh == 1, 17, 9)
    z_to = me + 2 - 4 * zh
    y_to = lax.rem(me + 16, n_seq)
    sib = me + 1 - 2 * core

    def x_to(j):
        return slab + lax.rem(me - slab + 16 - 4 * j, 16)

    def x_src(j, a, b):
        dest_x = lax.rem(xx + 4 - j, 4)
        return jnp.where(dest_x > xx, a, b)

    copy_z = packet(0, jnp.where(zh == 0, 9, 17), 0, z_to)
    copy_y0 = packet(0, 1, 1, y_to)
    copy_y1 = packet(a1, b1, 2, y_to)
    copies_x0 = [packet(x_src(j, 0, 1), 2 + j, 2 + j, x_to(j)) for j in (1, 2, 3)]
    copies_x1 = [packet(x_src(j, a1, b1), 10 + j, 5 + j, x_to(j)) for j in (1, 2, 3)]
    copy_c0 = packet(jnp.where(core == 0, 0, 1), 2, 9, sib)
    copy_c1 = packet(9, 10, 10, sib)
    copies_f0 = [packet(2 + j, 5 + j, 10 + j, sib) for j in (1, 2, 3)]
    copies_f1 = [packet(10 + j, 13 + j, 13 + j, sib) for j in (1, 2, 3)]

    def arrived(slot):
        pltpu.make_async_copy(kvb.at[slot], kvb.at[slot], kv_rsem.at[slot]).wait()

    copy_y0.start()
    copy_z.start()

    def values_of(slot, kv):
        lo = 0 if kv == 0 else 64
        return jnp.concatenate(
            [kvb[slot, 512 + j * 144 + lo : 512 + j * 144 + lo + 80, :] for j in range(4)], axis=1
        )

    for c in range(CHUNKS):
        span = (c + 1) * 128
        key_at = lax.broadcasted_iota(jnp.int32, (span, 128), 0).astype(F32)
        query_at = lax.broadcasted_iota(jnp.int32, (span, 128), 1).astype(F32) + c * 128
        allowed1 = (key_at <= query_at) & (key_at >= first[:, c * 128 : (c + 1) * 128])
        bias1 = jnp.where(allowed1, 0.0, -BIG)
        bias = jnp.concatenate([bias1, bias1, bias1, bias1], axis=1)
        for kv in range(2):
            lanes = slice(kv * 2048 + c * 512, kv * 2048 + c * 512 + 512)
            s = jnp.dot(kvb[0, 0:span, :], qt[0:128, lanes], preferred_element_type=F32) + bias
            top = jnp.max(s, axis=0, keepdims=True)
            p = jnp.exp2(s - top).astype(BF16)
            mx[:, lanes] = jnp.broadcast_to(top, (8, 512))
            acc[:, lanes] = jnp.dot(
                values_of(0, kv)[:, 0:span], p, preferred_element_type=F32
            )

    u_at = lax.broadcasted_iota(jnp.int32, (512, 128), 0).astype(F32)
    f_lane = lax.broadcasted_iota(jnp.int32, (512, 128), 1)

    def prepare(slot):
        strange = jnp.zeros((1, 128), F32)
        for j in range(4):
            aux = kvb[slot, 512 + j * 144 + 64 : 512 + j * 144 + 80, :].astype(F32)
            strange = strange + jnp.where(aux[1:2, :] != seg0, 1.0, 0.0)
        count = jnp.sum(strange, axis=1, keepdims=True)
        bias = jnp.where(u_at < count, -BIG, 0.0)
        kf[slot] = jnp.where(f_lane == 0, 1.0, jnp.where(f_lane == 1, bias, 0.0)).astype(BF16)

    def unit(slot, kv, start, width):
        lanes = pl.ds(start, width)
        q = qt[:, lanes]
        scores = []
        for s in (slot, slot + 1):
            k = jnp.concatenate([kvb[s, 0:512, :], kf[s]], axis=1)
            scores.append(jnp.dot(k, q, preferred_element_type=F32))
        old = mx[:, lanes]
        tops = [jnp.max(s, axis=0, keepdims=True) for s in scores]
        new = jnp.maximum(old, jnp.maximum(tops[0], tops[1]))
        factor = jnp.exp2(old - new)
        total = acc[:, lanes] * factor[0:1]
        for i, s in enumerate(scores):
            p = jnp.exp2(s - new[0:1]).astype(BF16)
            total = total + jnp.dot(values_of(slot + i, kv), p, preferred_element_type=F32)
        acc[:, lanes] = total
        mx[:, lanes] = new

    def arrive(i):
        first_slot = 2 * i + 1

        @pl.when(i == 0)
        def _():
            arrived(1)
            for copy in copies_x0:
                copy.start()
            copy_c0.start()

        @pl.when(i == 1)
        def _():
            arrived(a1)
            copy_y1.start()

        @pl.when(i == 2)
        def _():
            arrived(b1)
            for copy in copies_x1:
                copy.start()
            copy_c1.start()

        for j in range(2):
            slot = first_slot + j

            @pl.when((slot != 1) & (slot != 9))
            def _():
                arrived(slot)

            @pl.when(((slot >= 3) & (slot <= 5)) | ((slot >= 11) & (slot <= 13)))
            def _():
                late = jnp.where(slot >= 11, 1, 0)
                packet(slot, slot + 3, slot + 8 - 5 * late, sib).start()

            prepare(slot)

    def early(i, carry):
        arrive(i)
        for kv in range(2):
            unit(2 * i + 1, kv, kv * 2048, 2048)
        return carry

    lax.fori_loop(0, EARLY_PAIRS, early, 0)

    cp_wo.wait()

    def reduce_copy(c, k):
        return pltpu.make_async_remote_copy(
            src_ref=rs_send.at[c, k - 1],
            dst_ref=rs_recv.at[c, k - 1],
            send_sem=r_ssem.at[c, k - 1],
            recv_sem=r_rsem.at[c, k - 1],
            device_id={"seq": me, "tp": lax.rem(tp + k, n_tp)},
            device_id_type=MESH,
        )

    def square_copy(c, k):
        return pltpu.make_async_remote_copy(
            src_ref=ss_send.at[c],
            dst_ref=ss_recv.at[c, k - 1],
            send_sem=s_ssem.at[c, k - 1],
            recv_sem=s_rsem.at[c, k - 1],
            device_id={"seq": me, "tp": lax.rem(tp + k, n_tp)},
            device_id_type=MESH,
        )

    def late(c, carry):
        def step(i, inner):
            @pl.when(c == 0)
            def _():
                arrive(i)

            for kv in range(2):
                unit(2 * i + 1, kv, pl.multiple_of(kv * 2048 + c * 512, 512), 512)
            return inner

        lax.fori_loop(EARLY_PAIRS, PAIRS, step, 0)
        heads = []
        for kv in range(2):
            a = acc[:, pl.ds(pl.multiple_of(kv * 2048 + c * 512, 512), 512)]
            if kv == 0:
                o, den = a[0:64], a[64:65]
            else:
                o, den = a[16:80], a[0:1]
            o = o / den
            for pair in range(2):
                two = jnp.concatenate(
                    [
                        o[:, pair * 256 : pair * 256 + 128],
                        o[:, pair * 256 + 128 : pair * 256 + 256],
                    ],
                    axis=0,
                )
                heads.append(jnp.transpose(two).astype(BF16))
        attended = jnp.concatenate(heads, axis=1)
        rows = pl.ds(pl.multiple_of(c * 128, 128), 128)
        for k in (1, 2, 3, 0):
            col = pl.multiple_of(lax.rem(tp + k, n_tp) * 512, 512)
            part = jnp.dot(attended, wov[:, pl.ds(col, 512)], preferred_element_type=F32)
            if k == 0:
                resid[rows, :] = xv[rows, pl.ds(col, 512)].astype(F32) + part
            else:
                rs_send[c, k - 1] = part.astype(BF16)
                reduce_copy(c, k).start()
        return carry

    lax.fori_loop(0, CHUNKS, late, 0)

    def settle(c, carry):
        rows = pl.ds(pl.multiple_of(c * 128, 128), 128)
        total = resid[rows, :]
        for k in range(1, n_tp):
            reduce_copy(c, k).wait_recv()
            total = total + rs_recv[c, k - 1].astype(F32)
        resid[rows, :] = total
        hid_ref[rows, :] = total.astype(BF16)
        square = jnp.sum(total * total, axis=1, keepdims=True)
        ss_send[c] = jnp.transpose(jnp.broadcast_to(square, (128, 128)))[0:8]
        for k in range(1, n_tp):
            square_copy(c, k).start()
        return carry

    lax.fori_loop(0, CHUNKS, settle, 0)

    def finish(c, carry):
        rows = pl.ds(pl.multiple_of(c * 128, 128), 128)
        square = ss_send[c]
        for k in range(1, n_tp):
            square_copy(c, k).wait_recv()
            square = square + ss_recv[c, k - 1]
        column = jnp.transpose(jnp.broadcast_to(square[0:1], (128, 128)))
        scale = lax.rsqrt(column[:, 0:1] * (1.0 / 2048.0) + 1e-05)
        mlp_ref[rows, :] = (resid[rows, :] * scale * ogain_ref[...]).astype(BF16)
        for k in range(1, n_tp):
            reduce_copy(c, k).wait_send()
            square_copy(c, k).wait_send()
        return carry

    lax.fori_loop(0, CHUNKS, finish, 0)

    for copy in [copy_z, copy_y0, copy_y1, copy_c0, copy_c1]:
        copy.wait_send()
    for copy in copies_x0 + copies_x1 + copies_f0 + copies_f1:
        copy.wait_send()

    def cache_wait(k, carry):
        cache_copy(k).wait_send()
        cache_copy(k).wait_recv()
        return carry

    lax.fori_loop(1, n_seq, cache_wait, 0)
    cp_own.wait()


def per_device(
    n_seq,
    n_tp,
    tokens,
    norm_gain,
    query_key_value_weight,
    output_weight,
    out_gain,
    seg_ids,
    earlier_cache,
    decode_owner,
):
    tok, width = tokens.shape
    blocks = earlier_cache.shape[0]
    w = query_key_value_weight.reshape(width, -1)
    wo = output_weight.reshape(-1, width)
    owner = decode_owner[:, 0]
    index = jnp.arange(blocks, dtype=jnp.int32)
    same = (owner[:, None] == owner[None, :]) & (index[:, None] < index[None, :])
    slot = owner * 2 + jnp.sum(same.astype(jnp.int32), axis=0)
    hit = slot[None, :] == jnp.arange(2 * n_seq, dtype=jnp.int32)[:, None]
    inverse = jnp.min(jnp.where(hit, index[None, :], blocks), axis=1)
    rope = jnp.asarray(rope_tables(tok, n_seq))
    share = width // n_tp
    vmem = pl.BlockSpec(memory_space=pltpu.VMEM)
    hbm = pl.BlockSpec(memory_space=pl.ANY)
    smem = pl.BlockSpec(memory_space=pltpu.SMEM)
    dma = pltpu.SemaphoreType.DMA
    hidden, mlp, dec = pl.pallas_call(
        functools.partial(body, n_seq, n_tp),
        out_shape=(
            jax.ShapeDtypeStruct((tok, share), BF16),
            jax.ShapeDtypeStruct((tok, share), BF16),
            jax.ShapeDtypeStruct((2 * n_seq, 2, 2048), BF16),
        ),
        in_specs=[hbm, vmem, hbm, hbm, vmem, vmem, hbm, smem, vmem],
        out_specs=(vmem, vmem, hbm),
        scratch_shapes=[
            pltpu.VMEM((tok, width), BF16),
            pltpu.VMEM((width, 768), BF16),
            pltpu.VMEM((512, width), BF16),
            pltpu.VMEM((blocks + 1, 2, 2048), BF16),
            pltpu.VMEM((2 * n_seq, 2, 2048), BF16),
            pltpu.VMEM((18, PACKET_ROWS, 128), BF16),
            pltpu.VMEM((18, 512, 128), BF16),
            pltpu.VMEM((256, 4096), BF16),
            pltpu.VMEM((8, 4096), F32),
            pltpu.VMEM((80, 4096), F32),
            pltpu.VMEM((tok, share), F32),
            pltpu.VMEM((CHUNKS, 3, 128, share), BF16),
            pltpu.VMEM((CHUNKS, 3, 128, share), BF16),
            pltpu.VMEM((CHUNKS, 8, 128), F32),
            pltpu.VMEM((CHUNKS, 3, 8, 128), F32),
            dma((5,)),
            dma((64,)),
            dma((64,)),
            dma((17,)),
            dma((18,)),
            dma((CHUNKS, 3)),
            dma((CHUNKS, 3)),
            dma((CHUNKS, 3)),
            dma((CHUNKS, 3)),
        ],
        compiler_params=pltpu.CompilerParams(
            collective_id=0, has_side_effects=True, vmem_limit_bytes=58 << 20
        ),
        name="attention_block",
    )(
        tokens,
        norm_gain.reshape(1, -1),
        w,
        wo,
        out_gain.reshape(1, -1),
        seg_ids.reshape(1, -1),
        earlier_cache,
        inverse,
        rope,
    )
    return (hidden, mlp, dec)


def solution(mesh):
    n_seq, n_tp = mesh.shape["seq"], mesh.shape["tp"]
    in_specs = (
        P("seq", None),
        P(),
        P(None, "tp", None),
        P("tp", None, None),
        P("tp"),
        P("seq"),
        P("seq", "tp", None),
        P("seq", None),
    )
    out_specs = (P("seq", "tp"), P("seq", "tp"), P("seq", "tp", None))
    return jax.shard_map(
        functools.partial(per_device, n_seq, n_tp),
        mesh=mesh,
        in_specs=in_specs,
        out_specs=out_specs,
        check_vma=False,
    )
```

time: 600 us -> 150 us (0.25)
  starting transfers between devices: 334 us -> 0 us
  Pallas kernels: 0 us -> 136 us
  waiting for transfers between devices: 125 us -> 0 us
  local copies, waits for them, and re-layouts: 39.2 us -> 10.8 us
  blocking collectives: 24.5 us -> 0 us
  loops' own time: 22.3 us -> 0 us
  matrix products: 16.6 us -> 0 us
  other arithmetic: 17.5 us -> 2.09 us
  between operations: 15.5 us -> 0.64 us
    ppermute x32 -> x0, starting transfers between devices: 225 us -> none  [passed_along(): return lax.ppermute(value, axis, pairs)]
    pallas_call x0 -> x1, Pallas kernels: none -> 136 us  [per_device(): pl.pallas_call(functools.partial(body, n_seq, n_tp), out_shape=(jax.Shape...]
    all_to_all x1 -> x0, starting transfers between devices: 108 us -> none  [per_device(): lax.all_to_all(outgoing, 'seq', split_axis=0, concat_axis=0, tiled=True)]
    psum x1 -> x0, waiting for transfers between devices: 82.7 us -> none  [per_device(): lax.psum(projected_out.astype(jnp.bfloat16), 'tp').astype(jnp.float32)]
    all_to_all x1 -> x0, waiting for transfers between devices: 31.1 us -> none  [per_device(): lax.all_to_all(outgoing, 'seq', split_axis=0, concat_axis=0, tiled=True)]
    pmin x1 -> x0, blocking collectives: 24.5 us -> none  [per_device(): request_first = lax.pmin(local_first, 'seq')]
    another operation x18 -> x0, loops' own time: 22.3 us -> none  [the longest x1 21.8 us: per_device(): lax.fori_loop(0, reach_blocks, advance, (softmax_state, packed, seg_ids))]
    slice x35 -> x0, local copies, waits for them, and re-layouts: 20.6 us -> none  [the longest x17 9.79 us: absorb(): seg_ids[0]]
  transfers between devices with their start and end apart: 34 -> 0, of which waited for: 18 -> 0; matrix products, arithmetic and copies ran while one was open for 4% -> 0% of each run, Pallas kernels for 0% -> 0%
where the time goes in v1:
time: 150 us; the launch traced here: 149 us
  Pallas kernels  136 us (91%)
  local copies, waits for them, and re-layouts  10.8 us (7%)
  other arithmetic  2.09 us (1%)
    pallas_call x1, Pallas kernels, per_device(): pl.pallas_call(functools.partial(body, n_seq, n_tp), out_shape=(jax.Shape...  136 us
    unnamed x4, local copies, waits for them, and re-layouts  10.8 us

profile of v1, /device:TPU:2, one launch (start us, length us, event | category | flops | bytes accessed | tf_op | source)
XLA Modules:
  0.0 149.3 jit_solution(17256486414760652203)
XLA Ops:
  0.6 0.8 convert_reduce_fusion
  1.5 0.7 multiply_add_fusion
  2.1 0.6 select_reduce_fusion.inv_ref
  2.7 4.2 %copy.12 = bf16[256,8,2,384]{3,1,2,0:T(8,128)(2,1)} copy(bf16[256,8,2,384]{3,2,1,0:T(2,128)(2,1)} %bitcast.9) | data formatting | bytes 6291456
  6.9 135.7 %attention_block.1 = (bf16[512,512]{1,0:T(8,128)(2,1)}, bf16[512,512]{1,0:T(8,128)(2,1)}, bf16[128,2,2048]{2,1,0:T(2,128)(2,1)}) custom-call(bf16[512,2048]{1,0:T(8,128)(2,1)} %x_hbm.1, f32[1,2048]{1,0:T(1,128)} %bitcast.11, bf16[2048,768]{1,0:T(8,128)(2,1)} %bitcast.8, bf16[512,2048]{1,0:T(8,128)(2,1)} %bitcast.10, f32[1,512]{1,0:T(1,128)} %bitcast.12, ...), custom_call_target="tpu_custom_call" | custom-call | tf_op jit(solution)/shard_map/attention_block/pallas_call | solution.py:489
  142.6 1.9 %copy.16 = bf16[512,512]{1,0:T(8,128)(2,1)} copy(bf16[512,512]{1,0:T(8,128)(2,1)} %get-tuple-element.6) | data formatting | bytes 1048576
  144.5 1.9 %copy.17 = bf16[512,512]{1,0:T(8,128)(2,1)} copy(bf16[512,512]{1,0:T(8,128)(2,1)} %get-tuple-element.7) | data formatting | bytes 1048576
  146.4 2.9 %copy.18 = bf16[128,2,2048]{2,1,0:T(2,128)(2,1)} copy(bf16[128,2,2048]{2,1,0:T(2,128)(2,1)} %get-tuple-element.8) | data formatting | bytes 2097152

commit v2 on v1

v2 whole, which is shorter than its diff:
```python
import functools
import math

import jax
import jax.numpy as jnp
import numpy as np
from jax import lax
from jax.experimental import pallas as pl
from jax.experimental.pallas import tpu as pltpu
from jax.sharding import PartitionSpec as P

HEAD_SIZE = 64
QUERY_PER_KEY = 4
REQS = 16
BIG = float(2.0**100)
CHUNKS = 4
PACKET_ROWS = 256 + 4 * 80
PAIRS = 8
EARLY_PAIRS = (5, 2)
CACHE_AHEAD = 0
CACHE_STEP = 8
MESH = pl.DeviceIdType.MESH
F32 = jnp.float32
BF16 = jnp.bfloat16


def rope_tables(tok, blocks):
    half = HEAD_SIZE // 2
    freq = 500000.0 ** (-2.0 * np.arange(half) / HEAD_SIZE)
    inner = freq[:, None] * np.arange(tok)[None, :]
    outer = freq[:, None] * (np.arange(128) * tok)[None, :]
    parts = [np.cos(inner), np.sin(inner), np.cos(outer), np.sin(outer)]
    return np.concatenate(parts, axis=1).astype(np.float32)


def body(
    n_seq,
    n_tp,
    x_hbm,
    gain_ref,
    w_hbm,
    wo_hbm,
    ogain_ref,
    seg_ref,
    cache_hbm,
    inv_ref,
    rope_ref,
    hid_ref,
    mlp_ref,
    dec_hbm,
    xv,
    wv,
    wov,
    cachev,
    outg,
    kvb,
    kf,
    qt,
    mx,
    acc,
    resid,
    att,
    att_in,
    wg,
    ss_send,
    ss_recv,
    lsem,
    c_ssem,
    c_rsem,
    kv_ssem,
    kv_rsem,
    r_ssem,
    r_rsem,
    s_ssem,
    s_rsem,
    w_ssem,
    w_rsem,
):
    me = lax.axis_index("seq")
    tp = lax.axis_index("tp")
    core = lax.rem(me, 2)
    zh = lax.rem(me // 2, 2)
    xx = lax.rem(me // 4, 4)
    yy = me // 16
    slab = (me // 16) * 16
    tok = 512

    cp_cache = pltpu.make_async_copy(cache_hbm, cachev.at[pl.ds(0, 64)], lsem.at[0])
    cp_x = pltpu.make_async_copy(x_hbm, xv, lsem.at[1])
    cp_w = pltpu.make_async_copy(w_hbm, wv, lsem.at[2])
    cp_wo = pltpu.make_async_copy(wo_hbm, wov, lsem.at[3])
    cp_cache.start()
    cp_x.start()
    cp_w.start()
    cp_wo.start()

    barrier = pltpu.get_barrier_semaphore()

    def greet(k, carry):
        pl.semaphore_signal(
            barrier,
            inc=1,
            device_id={"seq": lax.rem(me + k, n_seq), "tp": tp},
            device_id_type=MESH,
        )
        return carry

    lax.fori_loop(1, n_seq, greet, 0)
    for k in range(1, n_tp):
        pl.semaphore_signal(
            barrier,
            inc=1,
            device_id={"seq": me, "tp": lax.rem(tp + k, n_tp)},
            device_id_type=MESH,
        )

    cachev[64] = jnp.zeros((2, 2048), BF16)
    cp_cache.wait()

    def place(r, carry):
        outg[r] = cachev[inv_ref[r]]
        return carry

    lax.fori_loop(0, 2 * n_seq, place, 0)
    pl.semaphore_wait(barrier, n_seq - 1 + n_tp - 1)

    def cache_copy(k):
        to_y = lax.rem(yy + lax.rem(k, 32) // 8, 4)
        to_x = lax.rem(xx + lax.rem(k, 8) // 2, 4)
        to_z = lax.rem(zh + k // 32, 2)
        to_c = lax.rem(core + lax.rem(k, 2), 2)
        to = ((to_y * 4 + to_x) * 2 + to_z) * 2 + to_c
        return pltpu.make_async_remote_copy(
            src_ref=outg.at[pl.ds(2 * to, 2)],
            dst_ref=dec_hbm.at[pl.ds(2 * me, 2)],
            send_sem=c_ssem.at[k],
            recv_sem=c_rsem.at[k],
            device_id={"seq": to, "tp": tp},
            device_id_type=MESH,
        )

    def cache_start(k, carry):
        cache_copy(k).start()
        return carry

    cp_own = pltpu.make_async_copy(
        outg.at[pl.ds(2 * me, 2)], dec_hbm.at[pl.ds(2 * me, 2)], lsem.at[4]
    )
    cp_own.start()

    share_at = core * 16 + yy * 4 + xx

    def weight_z(k):
        to = lax.rem(tp + k, n_tp)
        return pltpu.make_async_remote_copy(
            src_ref=wov.at[
                pl.ds(pl.multiple_of(share_at * 16, 16), 16),
                pl.ds(pl.multiple_of(to * 512, 512), 512),
            ],
            dst_ref=wg.at[share_at, k - 1],
            send_sem=w_ssem.at[k - 1],
            recv_sem=w_rsem.at[k - 1],
            device_id={"seq": me, "tp": to},
            device_id_type=MESH,
        )

    def weight_part(at, count, sem, to):
        return pltpu.make_async_remote_copy(
            src_ref=wg.at[pl.ds(at, count)],
            dst_ref=wg.at[pl.ds(at, count)],
            send_sem=w_ssem.at[sem],
            recv_sem=w_rsem.at[sem],
            device_id={"seq": to, "tp": tp},
            device_id_type=MESH,
        )

    weights_z = [weight_z(k) for k in (1, 2, 3)]
    weights_x = [
        weight_part(share_at, 1, 2 + j, slab + lax.rem(me - slab + 4 * j, 16)) for j in (1, 2, 3)
    ]
    weights_y = [
        weight_part(core * 16 + yy * 4, 4, 5 + j, lax.rem(me + 16 * j, n_seq)) for j in (1, 2, 3)
    ]
    weight_c = weight_part(core * 16, 16, 9, me + 1 - 2 * core)
    cp_wo.wait()
    for copy in weights_z:
        copy.start()
    lax.fori_loop(1, 32, cache_start, 0)

    lane = lax.broadcasted_iota(jnp.int32, (32, 128), 1)
    here = lane == me
    cos_b = jnp.sum(jnp.where(here, rope_ref[:, 2 * tok : 2 * tok + 128], 0.0), axis=1, keepdims=True)
    sin_b = jnp.sum(
        jnp.where(here, rope_ref[:, 2 * tok + 128 : 2 * tok + 256], 0.0), axis=1, keepdims=True
    )
    q_scale = HEAD_SIZE ** (-0.5) * math.log2(math.e)

    seg = seg_ref[...].astype(F32)
    seg0 = jnp.min(seg, axis=1, keepdims=True)
    carried_in = seg == seg0
    first = jnp.zeros((1, tok), F32)
    for r in range(1, REQS):
        below = jnp.sum(jnp.where(seg < r, 1.0, 0.0), axis=1, keepdims=True)
        first = jnp.where(seg == r, below, first)
    a_bias = jnp.where(carried_in, 0.0, -BIG)

    row16 = lax.broadcasted_iota(jnp.int32, (16, 512), 0)
    for c in range(CHUNKS):
        ab = a_bias[:, c * 128 : (c + 1) * 128]
        ab4 = jnp.concatenate([ab, ab, ab, ab], axis=1)
        feat = jnp.where(row16 == 0, ab4, jnp.where(row16 == 1, 1.0, 0.0)).astype(BF16)
        for kv in range(2):
            lanes = slice(kv * 2048 + c * 512, kv * 2048 + c * 512 + 512)
            for half in range(2):
                qt[half, 128:144, lanes] = feat
                qt[half, 144:256, lanes] = jnp.zeros((112, 512), BF16)
                qt[half, (1 - half) * 64 : (1 - half) * 64 + 64, lanes] = jnp.zeros((64, 512), BF16)

    cp_x.wait()
    cp_w.wait()
    gain = gain_ref[...]
    aux_row = lax.broadcasted_iota(jnp.int32, (16, 128), 0)
    keys_t = [[None] * CHUNKS, [None] * CHUNKS]
    for c in range(CHUNKS):
        cols = slice(c * 128, (c + 1) * 128)
        xc = xv[cols, :].astype(F32)
        ms = jnp.mean(xc * xc, axis=1, keepdims=True)
        normed = (xc * lax.rsqrt(ms + 1e-05) * gain).astype(BF16)
        proj = jnp.dot(normed, wv[...], preferred_element_type=F32)
        ci = rope_ref[:, c * 128 : (c + 1) * 128]
        si = rope_ref[:, tok + c * 128 : tok + (c + 1) * 128]
        cos = ci * cos_b - si * sin_b
        sin = si * cos_b + ci * sin_b
        cos_q, sin_q = cos * q_scale, sin * q_scale

        def rot(a, co, sn):
            a1, a2 = a[0:32], a[32:64]
            return jnp.concatenate([a1 * co - a2 * sn, a2 * co + a1 * sn], axis=0)

        for kv in range(2):
            for pair in range(2):
                at = kv * 384 + pair * 128
                tr = jnp.transpose(proj[:, at : at + 128])
                for g2 in range(2):
                    g = pair * 2 + g2
                    lane0 = kv * 2048 + c * 512 + g * 128
                    q = rot(tr[g2 * 64 : g2 * 64 + 64], cos_q, sin_q).astype(BF16)
                    qt[0, 0:64, lane0 : lane0 + 128] = q
                    qt[1, 64:128, lane0 : lane0 + 128] = q
            tr = jnp.transpose(proj[:, kv * 384 + 256 : kv * 384 + 384])
            keys_t[kv][c] = rot(tr[0:64], cos, sin)
            base = 256 + c * 80
            kvb[kv * 18, base : base + 64, :] = tr[64:128].astype(BF16)
            kvb[kv * 18, base + 64 : base + 80, :] = jnp.where(
                aux_row == 0, 1.0, jnp.where(aux_row == 1, seg[:, cols], 0.0)
            ).astype(BF16)
    for kv in range(2):
        for j in range(2):
            kvb[kv * 18, j * 128 : (j + 1) * 128, :] = jnp.transpose(
                jnp.concatenate([keys_t[kv][j], keys_t[kv][j + 2]], axis=0)
            ).astype(BF16)

    def packet(h, src, dst, sem, seq_to):
        return pltpu.make_async_remote_copy(
            src_ref=kvb.at[18 * h + src],
            dst_ref=kvb.at[18 * h + dst],
            send_sem=kv_ssem.at[17 * h + sem],
            recv_sem=kv_rsem.at[18 * h + dst],
            device_id={"seq": seq_to, "tp": tp},
            device_id_type=MESH,
        )

    a1 = jnp.where(zh == 1, 9, 17)
    b1 = jnp.where(zh == 1, 17, 9)
    z_to = me + 2 - 4 * zh
    y_to = lax.rem(me + 16, n_seq)
    sib = me + 1 - 2 * core

    def x_to(j):
        return slab + lax.rem(me - slab + 16 - 4 * j, 16)

    def x_src(j, a, b):
        dest_x = lax.rem(xx + 4 - j, 4)
        return jnp.where(dest_x > xx, a, b)

    def copy_z(h):
        return packet(h, 0, jnp.where(zh == 0, 9, 17), 0, z_to)

    def copy_y0(h):
        return packet(h, 0, 1, 1, y_to)

    def copy_y1(h):
        return packet(h, a1, b1, 2, y_to)

    def copies_x0(h):
        return [packet(h, x_src(j, 0, 1), 2 + j, 2 + j, x_to(j)) for j in (1, 2, 3)]

    def copies_x1(h):
        return [packet(h, x_src(j, a1, b1), 10 + j, 5 + j, x_to(j)) for j in (1, 2, 3)]

    def copy_c0(h):
        return packet(h, jnp.where(core == 0, 0, 1), 2, 9, sib)

    def copy_c1(h):
        return packet(h, 9, 10, 10, sib)

    def copies_f0(h):
        return [packet(h, 2 + j, 5 + j, 10 + j, sib) for j in (1, 2, 3)]

    def copies_f1(h):
        return [packet(h, 10 + j, 13 + j, 13 + j, sib) for j in (1, 2, 3)]

    def arrived(h, slot):
        here_at = kvb.at[18 * h + slot]
        pltpu.make_async_copy(here_at, here_at, kv_rsem.at[18 * h + slot]).wait()

    for h in range(2):
        copy_y0(h).start()
        copy_z(h).start()
    for copy in weights_z:
        copy.wait_recv()
    for copy in weights_x:
        copy.start()

    def values_of(h, slot, half):
        at = 256 + half * 160
        return jnp.concatenate(
            [kvb[18 * h + slot, at : at + 80, :], kvb[18 * h + slot, at + 80 : at + 160, :]], axis=1
        )

    for c in range(CHUNKS):
        span = (c + 1) * 128
        key_at = lax.broadcasted_iota(jnp.int32, (span, 128), 0).astype(F32)
        query_at = lax.broadcasted_iota(jnp.int32, (span, 128), 1).astype(F32) + c * 128
        allowed1 = (key_at <= query_at) & (key_at >= first[:, c * 128 : (c + 1) * 128])
        bias1 = jnp.where(allowed1, 0.0, -BIG)
        bias = jnp.concatenate([bias1, bias1, bias1, bias1], axis=1)
        for kv in range(2):
            lanes = slice(kv * 2048 + c * 512, kv * 2048 + c * 512 + 512)
            parts = [
                jnp.dot(
                    kvb[18 * kv, 0 : min(span, 256), :],
                    qt[0, 0:128, lanes],
                    preferred_element_type=F32,
                )
            ]
            vals = [values_of(kv, 0, 0)]
            if span > 256:
                parts.append(
                    jnp.dot(
                        kvb[18 * kv, 0 : span - 256, :],
                        qt[1, 0:128, lanes],
                        preferred_element_type=F32,
                    )
                )
                vals.append(values_of(kv, 0, 1))
            s = jnp.concatenate(parts, axis=0) + bias
            top = jnp.max(s, axis=0, keepdims=True)
            p = jnp.exp2(s - top).astype(BF16)
            mx[:, lanes] = jnp.broadcast_to(top, (8, 512))
            acc[:, lanes] = jnp.dot(
                jnp.concatenate(vals, axis=1)[:, 0:span], p, preferred_element_type=F32
            )

    u_at = lax.broadcasted_iota(jnp.int32, (512, 128), 0).astype(F32)
    f_lane = lax.broadcasted_iota(jnp.int32, (512, 128), 1)

    def prepare(slot):
        strange = jnp.zeros((1, 128), F32)
        for j in range(4):
            aux = kvb[slot, 256 + j * 80 + 64 : 256 + j * 80 + 80, :].astype(F32)
            strange = strange + jnp.where(aux[1:2, :] != seg0, 1.0, 0.0)
        count = jnp.sum(strange, axis=1, keepdims=True)
        bias = jnp.where(u_at < count, -BIG, 0.0)
        kf[slot] = jnp.where(f_lane == 0, 1.0, jnp.where(f_lane == 1, bias, 0.0)).astype(BF16)

    def unit(slot, h, start, width):
        lanes = pl.ds(start, width)
        scores, vals = [], []
        for half in range(2):
            k = jnp.concatenate(
                [
                    jnp.concatenate(
                        [kvb[18 * h + s, 0:256, :], kf[s, half * 256 : half * 256 + 256, :]], axis=1
                    )
                    for s in (slot, slot + 1)
                ],
                axis=0,
            )
            scores.append(jnp.dot(k, qt[half, :, lanes], preferred_element_type=F32))
            vals.append(
                jnp.concatenate([values_of(h, slot, half), values_of(h, slot + 1, half)], axis=1)
            )
        old = mx[:, lanes]
        tops = [jnp.max(s, axis=0, keepdims=True) for s in scores]
        new = jnp.maximum(old, jnp.maximum(tops[0], tops[1]))
        factor = jnp.exp2(old - new)
        total = acc[:, lanes] * factor[0:1]
        for s, v in zip(scores, vals):
            p = jnp.exp2(s - new[0:1]).astype(BF16)
            total = total + jnp.dot(v, p, preferred_element_type=F32)
        acc[:, lanes] = total
        mx[:, lanes] = new

    def spread(h):
        arrived(h, 1)
        for copy in copies_x0(h):
            copy.start()
        copy_c0(h).start()

    def spread_y(h):
        arrived(h, a1)
        copy_y1(h).start()

    def spread_late(h):
        arrived(h, b1)
        for copy in copies_x1(h):
            copy.start()
        copy_c1(h).start()

    def attended_copy(piece, k):
        return pltpu.make_async_remote_copy(
            src_ref=att.at[piece],
            dst_ref=att_in.at[piece, k - 1],
            send_sem=r_ssem.at[piece, k - 1],
            recv_sem=r_rsem.at[piece, k - 1],
            device_id={"seq": me, "tp": lax.rem(tp + k, n_tp)},
            device_id_type=MESH,
        )

    def conclude(h, c):
        a = acc[:, pl.ds(pl.multiple_of(h * 2048 + c * 512, 512), 512)]
        o = a[0:64] / a[64:65]
        for pair in range(2):
            two = jnp.concatenate(
                [o[:, pair * 256 : pair * 256 + 128], o[:, pair * 256 + 128 : pair * 256 + 256]],
                axis=0,
            )
            att[h * 4 + c, :, pair * 128 : pair * 128 + 128] = jnp.transpose(two).astype(BF16)
        for k in (2, 3, 1):
            attended_copy(h * 4 + c, k).start()

    def arrive0(i):
        @pl.when(i == 0)
        def _():
            spread(0)

        @pl.when(i == 1)
        def _():
            spread(1)
            spread_y(0)

        @pl.when(i == 2)
        def _():
            spread_late(0)
            for copy in weights_x:
                copy.wait_recv()
            for copy in weights_y:
                copy.start()

        @pl.when(i == 3)
        def _():
            spread_y(1)

        @pl.when(i == 4)
        def _():
            for slot in (3, 4, 5):
                arrived(1, slot)
            for copy in copies_f0(1):
                copy.start()

        @pl.when(i == 5)
        def _():
            spread_late(1)

        for j in range(2):
            slot = 2 * i + 1 + j

            @pl.when((slot != 1) & (slot != 9))
            def _():
                arrived(0, slot)

            @pl.when(((slot >= 3) & (slot <= 5)) | ((slot >= 11) & (slot <= 13)))
            def _():
                wave = jnp.where(slot >= 11, 1, 0)
                packet(0, slot, slot + 3, slot + 8 - 5 * wave, sib).start()

            prepare(slot)

        @pl.when((i >= 3) & (i <= 6))
        def _():
            at = 32 + CACHE_AHEAD + (i - 3) * CACHE_STEP
            lax.fori_loop(at, at + CACHE_STEP, cache_start, 0)

    def early0(i, carry):
        arrive0(i)
        unit(2 * i + 1, 0, 0, 2048)
        return carry

    lax.fori_loop(0, EARLY_PAIRS[0], early0, 0)

    def late0(c, carry):
        def step(i, inner):
            @pl.when(c == 0)
            def _():
                arrive0(i)

            unit(2 * i + 1, 0, pl.multiple_of(c * 512, 512), 512)
            return inner

        lax.fori_loop(EARLY_PAIRS[0], PAIRS, step, 0)
        conclude(0, c)
        return carry

    lax.fori_loop(0, CHUNKS, late0, 0)

    def arrive1(i):
        @pl.when(i == 0)
        def _():
            for copy in weights_y:
                copy.wait_recv()
            weight_c.start()

        @pl.when(i == 1)
        def _():
            for slot in (11, 12, 13):
                arrived(1, slot)
            for copy in copies_f1(1):
                copy.start()

        for j in range(2):
            slot = 2 * i + 1 + j

            @pl.when(
                (slot == 2)
                | (slot == 10)
                | ((slot >= 6) & (slot <= 8))
                | ((slot >= 14) & (slot <= 16))
            )
            def _():
                arrived(1, slot)

    def early1(i, carry):
        arrive1(i)
        unit(2 * i + 1, 1, 2048, 2048)
        return carry

    lax.fori_loop(0, EARLY_PAIRS[1], early1, 0)

    def square_copy(c, k):
        return pltpu.make_async_remote_copy(
            src_ref=ss_send.at[c],
            dst_ref=ss_recv.at[c, k - 1],
            send_sem=s_ssem.at[c, k - 1],
            recv_sem=s_rsem.at[c, k - 1],
            device_id={"seq": me, "tp": lax.rem(tp + k, n_tp)},
            device_id_type=MESH,
        )

    own_col = pl.ds(pl.multiple_of(tp * 512, 512), 512)

    def weight_of(k, h):
        if k == 0:
            return wov[h * 256 : h * 256 + 256, own_col]
        return jnp.concatenate([wg[h * 16 + e, k - 1] for e in range(16)], axis=0)

    def first_half():
        for k in range(1, n_tp):
            for c in range(CHUNKS):
                attended_copy(c, k).wait_recv()
        weight_c.wait_recv()
        total = xv[:, own_col].astype(F32)
        for k in range(n_tp):
            a = jnp.concatenate(
                [att[c] if k == 0 else att_in[c, k - 1] for c in range(CHUNKS)], axis=0
            )
            total = total + jnp.dot(a, weight_of(k, 0), preferred_element_type=F32)
        resid[...] = total

    def settle(c):
        rows = pl.ds(pl.multiple_of(c * 128, 128), 128)
        total = resid[rows, :]
        for k in range(n_tp):
            if k > 0:
                attended_copy(4 + c, k).wait_recv()
            a = att[4 + c] if k == 0 else att_in[4 + c, k - 1]
            total = total + jnp.dot(a, weight_of(k, 1), preferred_element_type=F32)
        resid[rows, :] = total
        hid_ref[rows, :] = total.astype(BF16)
        square = jnp.sum(total * total, axis=1, keepdims=True)
        ss_send[c] = jnp.transpose(jnp.broadcast_to(square, (128, 128)))[0:8]
        for k in range(1, n_tp):
            square_copy(c, k).start()

    def late(c, carry):
        def step(i, inner):
            @pl.when(c == 0)
            def _():
                arrive1(i)

            unit(2 * i + 1, 1, pl.multiple_of(2048 + c * 512, 512), 512)
            return inner

        lax.fori_loop(EARLY_PAIRS[1], PAIRS, step, 0)
        conclude(1, c)

        @pl.when(c == 1)
        def _():
            first_half()

        @pl.when(c > 0)
        def _():
            settle(c - 1)

        return carry

    lax.fori_loop(0, CHUNKS, late, 0)
    settle(CHUNKS - 1)

    def finish(c, carry):
        rows = pl.ds(pl.multiple_of(c * 128, 128), 128)
        square = ss_send[c]
        for k in range(1, n_tp):
            square_copy(c, k).wait_recv()
            square = square + ss_recv[c, k - 1]
        column = jnp.transpose(jnp.broadcast_to(square[0:1], (128, 128)))
        scale = lax.rsqrt(column[:, 0:1] * (1.0 / 2048.0) + 1e-05)
        mlp_ref[rows, :] = (resid[rows, :] * scale * ogain_ref[...]).astype(BF16)
        for k in range(1, n_tp):
            attended_copy(c, k).wait_send()
            attended_copy(4 + c, k).wait_send()
            square_copy(c, k).wait_send()
        return carry

    lax.fori_loop(0, CHUNKS, finish, 0)

    for h in range(2):
        for copy in [copy_z(h), copy_y0(h), copy_y1(h), copy_c0(h), copy_c1(h)]:
            copy.wait_send()
        for copy in copies_x0(h) + copies_x1(h) + copies_f0(h) + copies_f1(h):
            copy.wait_send()
    for copy in weights_z + weights_x + weights_y + [weight_c]:
        copy.wait_send()

    def cache_wait(k, carry):
        cache_copy(k).wait_send()
        cache_copy(k).wait_recv()
        return carry

    lax.fori_loop(1, n_seq, cache_wait, 0)
    cp_own.wait()


def hand_over(hid, mlp, dec, hid_out, mlp_out, dec_out, sems):
    pieces = [(hid, hid_out, 0), (mlp, mlp_out, 1)]
    copies = [pltpu.make_async_copy(a, b, sems.at[k]) for a, b, k in pieces]
    for k in range(4):
        rows = pl.ds(32 * k, 32)
        copies.append(pltpu.make_async_copy(dec.at[rows], dec_out.at[rows], sems.at[2 + k]))
    for copy in copies:
        copy.start()
    for copy in copies:
        copy.wait()


def per_device(
    n_seq,
    n_tp,
    tokens,
    norm_gain,
    query_key_value_weight,
    output_weight,
    out_gain,
    seg_ids,
    earlier_cache,
    decode_owner,
):
    tok, width = tokens.shape
    blocks = earlier_cache.shape[0]
    w = query_key_value_weight.reshape(width, -1)
    wo = output_weight.reshape(-1, width)
    owner = decode_owner[:, 0]
    index = jnp.arange(blocks, dtype=jnp.int32)
    same = (owner[:, None] == owner[None, :]) & (index[:, None] < index[None, :])
    slot = owner * 2 + jnp.sum(same.astype(jnp.int32), axis=0)
    hit = slot[None, :] == jnp.arange(2 * n_seq, dtype=jnp.int32)[:, None]
    inverse = jnp.min(jnp.where(hit, index[None, :], blocks), axis=1)
    rope = jnp.asarray(rope_tables(tok, n_seq))
    share = width // n_tp
    vmem = pl.BlockSpec(memory_space=pltpu.VMEM)
    hbm = pl.BlockSpec(memory_space=pl.ANY)
    smem = pl.BlockSpec(memory_space=pltpu.SMEM)
    dma = pltpu.SemaphoreType.DMA
    hidden, mlp, dec = pl.pallas_call(
        functools.partial(body, n_seq, n_tp),
        out_shape=(
            jax.ShapeDtypeStruct((tok, share), BF16),
            jax.ShapeDtypeStruct((tok, share), BF16),
            jax.ShapeDtypeStruct((2 * n_seq, 2, 2048), BF16),
        ),
        in_specs=[hbm, vmem, hbm, hbm, vmem, vmem, hbm, smem, vmem],
        out_specs=(vmem, vmem, hbm),
        scratch_shapes=[
            pltpu.VMEM((tok, width), BF16),
            pltpu.VMEM((width, 768), BF16),
            pltpu.VMEM((512, width), BF16),
            pltpu.VMEM((blocks + 1, 2, 2048), BF16),
            pltpu.VMEM((2 * n_seq, 2, 2048), BF16),
            pltpu.VMEM((36, PACKET_ROWS, 128), BF16),
            pltpu.VMEM((18, 512, 128), BF16),
            pltpu.VMEM((2, 256, 4096), BF16),
            pltpu.VMEM((8, 4096), F32),
            pltpu.VMEM((80, 4096), F32),
            pltpu.VMEM((tok, share), F32),
            pltpu.VMEM((2 * CHUNKS, 128, 256), BF16),
            pltpu.VMEM((2 * CHUNKS, 3, 128, 256), BF16),
            pltpu.VMEM((32, 3, 16, share), BF16),
            pltpu.VMEM((CHUNKS, 8, 128), F32),
            pltpu.VMEM((CHUNKS, 3, 8, 128), F32),
            dma((5,)),
            dma((64,)),
            dma((64,)),
            dma((34,)),
            dma((36,)),
            dma((2 * CHUNKS, 3)),
            dma((2 * CHUNKS, 3)),
            dma((CHUNKS, 3)),
            dma((CHUNKS, 3)),
            dma((10,)),
            dma((10,)),
        ],
        compiler_params=pltpu.CompilerParams(
            collective_id=0, has_side_effects=True, vmem_limit_bytes=58 << 20
        ),
        name="attention_block",
    )(
        tokens,
        norm_gain.reshape(1, -1),
        w,
        wo,
        out_gain.reshape(1, -1),
        seg_ids.reshape(1, -1),
        earlier_cache,
        inverse,
        rope,
    )
    return pl.pallas_call(
        hand_over,
        out_shape=(
            jax.ShapeDtypeStruct((tok, share), BF16),
            jax.ShapeDtypeStruct((tok, share), BF16),
            jax.ShapeDtypeStruct((2 * n_seq, 2, 2048), BF16),
        ),
        in_specs=[hbm, hbm, hbm],
        out_specs=(hbm, hbm, hbm),
        scratch_shapes=[dma((6,))],
        name="hand_over",
    )(hidden, mlp, dec)


def solution(mesh):
    n_seq, n_tp = mesh.shape["seq"], mesh.shape["tp"]
    in_specs = (
        P("seq", None),
        P(),
        P(None, "tp", None),
        P("tp", None, None),
        P("tp"),
        P("seq"),
        P("seq", "tp", None),
        P("seq", None),
    )
    out_specs = (P("seq", "tp"), P("seq", "tp"), P("seq", "tp", None))
    return jax.shard_map(
        functools.partial(per_device, n_seq, n_tp),
        mesh=mesh,
        in_specs=in_specs,
        out_specs=out_specs,
        check_vma=False,
    )
```

time: 150 us -> 197 us (1.31)
  Pallas kernels: 136 us -> 190 us
  local copies, waits for them, and re-layouts: 10.8 us -> 4.19 us
    pallas_call x0 -> x1, Pallas kernels: none -> 64.7 us  [per_device(): pl.pallas_call(hand_over, out_shape=(jax.ShapeDtypeStruct((tok, share), B...]
    pallas_call x1, Pallas kernels: 136 us -> 125 us  [per_device(): pl.pallas_call(functools.partial(body, n_seq, n_tp), out_shape=(jax.Shape...]
    unnamed x4 -> x1, local copies, waits for them, and re-layouts: 10.8 us -> 4.19 us
where the time goes in v2:
time: 197 us
  Pallas kernels  190 us (96%)
  local copies, waits for them, and re-layouts  4.19 us (2%)
  other arithmetic  2.09 us (1%)
    pallas_call x1, Pallas kernels, per_device(): pl.pallas_call(functools.partial(body, n_seq, n_tp), out_shape=(jax.Shape...  125 us
    pallas_call x1, Pallas kernels, per_device(): pl.pallas_call(hand_over, out_shape=(jax.ShapeDtypeStruct((tok, share), B...  64.7 us
    unnamed x1, local copies, waits for them, and re-layouts  4.19 us

profile of v2, /device:TPU:2, one launch (start us, length us, event | category | flops | bytes accessed | tf_op | source)
XLA Modules:
  0.0 197.2 jit_solution(7151280851760438776)
XLA Ops:
  0.6 0.8 convert_reduce_fusion
  1.5 0.7 multiply_add_fusion
  2.1 0.6 select_reduce_fusion.inv_ref
  2.7 4.2 %copy.12 = bf16[256,8,2,384]{3,1,2,0:T(8,128)(2,1)} copy(bf16[256,8,2,384]{3,2,1,0:T(2,128)(2,1)} %bitcast.9) | data formatting | bytes 6291456
  6.9 125.4 %attention_block.1 = (bf16[512,512]{1,0:T(8,128)(2,1)}, bf16[512,512]{1,0:T(8,128)(2,1)}, bf16[128,2,2048]{2,1,0:T(2,128)(2,1)}) custom-call(bf16[512,2048]{1,0:T(8,128)(2,1)} %x_hbm.1, f32[1,2048]{1,0:T(1,128)} %bitcast.11, bf16[2048,768]{1,0:T(8,128)(2,1)} %bitcast.8, bf16[512,2048]{1,0:T(8,128)(2,1)} %bitcast.10, f32[1,512]{1,0:T(1,128)} %bitcast.12, ...), custom_call_target="tpu_custom_call" | custom-call | tf_op jit(solution)/shard_map/attention_block/pallas_call | solution.py:694
  132.3 64.7 %hand_over.1 = (bf16[512,512]{1,0:T(8,128)(2,1)}, bf16[512,512]{1,0:T(8,128)(2,1)}, bf16[128,2,2048]{2,1,0:T(2,128)(2,1)}) custom-call(bf16[512,512]{1,0:T(8,128)(2,1)} %get-tuple-element.6.hid, bf16[512,512]{1,0:T(8,128)(2,1)} %get-tuple-element.7.mlp, bf16[128,2,2048]{2,1,0:T(2,128)(2,1)} %get-tuple-element.8.dec), custom_call_target="tpu_custom_call" | custom-call | tf_op jit(solution)/shard_map/hand_over/pallas_call | solution.py:747

commit v3 on v2

--- a/solution.py
+++ b/solution.py
@@ -651,15 +651,20 @@
     cp_own.wait()
 
 
-def hand_over(hid, mlp, dec, hid_out, mlp_out, dec_out, sems):
-    pieces = [(hid, hid_out, 0), (mlp, mlp_out, 1)]
-    copies = [pltpu.make_async_copy(a, b, sems.at[k]) for a, b, k in pieces]
+def hand_over(hid, mlp, dec, hid_out, mlp_out, dec_out, hid_v, mlp_v, dec_v, in_sems, out_sems):
+    pieces = [(hid, hid_v, hid_out), (mlp, mlp_v, mlp_out)]
+    step = dec.shape[0] // 4
     for k in range(4):
-        rows = pl.ds(32 * k, 32)
-        copies.append(pltpu.make_async_copy(dec.at[rows], dec_out.at[rows], sems.at[2 + k]))
-    for copy in copies:
+        rows = pl.ds(step * k, step)
+        pieces.append((dec.at[rows], dec_v.at[rows], dec_out.at[rows]))
+    ins = [pltpu.make_async_copy(a, v, in_sems.at[k]) for k, (a, v, b) in enumerate(pieces)]
+    outs = [pltpu.make_async_copy(v, b, out_sems.at[k]) for k, (a, v, b) in enumerate(pieces)]
+    for copy in ins:
         copy.start()
-    for copy in copies:
+    for first, second in zip(ins, outs):
+        first.wait()
+        second.start()
+    for copy in outs:
         copy.wait()
 
 
@@ -753,7 +758,13 @@
         ),
         in_specs=[hbm, hbm, hbm],
         out_specs=(hbm, hbm, hbm),
-        scratch_shapes=[dma((6,))],
+        scratch_shapes=[
+            pltpu.VMEM((tok, share), BF16),
+            pltpu.VMEM((tok, share), BF16),
+            pltpu.VMEM((2 * n_seq, 2, 2048), BF16),
+            dma((6,)),
+            dma((6,)),
+        ],
         name="hand_over",
     )(hidden, mlp, dec)
 

time: 197 us -> 135 us (0.69)
  Pallas kernels: 190 us -> 128 us
    pallas_call x1, Pallas kernels: 64.7 us -> 2.45 us  [per_device(): pl.pallas_call(hand_over, out_shape=(jax.ShapeDtypeStruct((tok, share), B...]
where the time goes in v3:
time: 135 us
  Pallas kernels  128 us (95%)
  local copies, waits for them, and re-layouts  4.19 us (3%)
  other arithmetic  2.09 us (2%)
    pallas_call x1, Pallas kernels, per_device(): pl.pallas_call(functools.partial(body, n_seq, n_tp), out_shape=(jax.Shape...  125 us
    unnamed x1, local copies, waits for them, and re-layouts  4.19 us

profile of v3, /device:TPU:2, one launch (start us, length us, event | category | flops | bytes accessed | tf_op | source)
XLA Modules:
  0.0 135.0 jit_solution(2922686697061147459)
XLA Ops:
  0.6 0.8 convert_reduce_fusion
  1.5 0.7 multiply_add_fusion
  2.1 0.6 select_reduce_fusion.inv_ref
  2.7 4.2 %copy.12 = bf16[256,8,2,384]{3,1,2,0:T(8,128)(2,1)} copy(bf16[256,8,2,384]{3,2,1,0:T(2,128)(2,1)} %bitcast.9) | data formatting | bytes 6291456
  6.9 125.4 %attention_block.1 = (bf16[512,512]{1,0:T(8,128)(2,1)}, bf16[512,512]{1,0:T(8,128)(2,1)}, bf16[128,2,2048]{2,1,0:T(2,128)(2,1)}) custom-call(bf16[512,2048]{1,0:T(8,128)(2,1)} %x_hbm.1, f32[1,2048]{1,0:T(1,128)} %bitcast.11, bf16[2048,768]{1,0:T(8,128)(2,1)} %bitcast.8, bf16[512,2048]{1,0:T(8,128)(2,1)} %bitcast.10, f32[1,512]{1,0:T(1,128)} %bitcast.12, ...), custom_call_target="tpu_custom_call" | custom-call | tf_op jit(solution)/shard_map/attention_block/pallas_call | solution.py:699
  132.3 2.5 %hand_over.1 = (bf16[512,512]{1,0:T(8,128)(2,1)}, bf16[512,512]{1,0:T(8,128)(2,1)}, bf16[128,2,2048]{2,1,0:T(2,128)(2,1)}) custom-call(bf16[512,512]{1,0:T(8,128)(2,1)} %get-tuple-element.6.hid, bf16[512,512]{1,0:T(8,128)(2,1)} %get-tuple-element.7.mlp, bf16[128,2,2048]{2,1,0:T(2,128)(2,1)} %get-tuple-element.8.dec), custom_call_target="tpu_custom_call" | custom-call | tf_op jit(solution)/shard_map/hand_over/pallas_call | solution.py:752
